TPU v7x, 256 devices: a whole 4x4x8 slice. The times are simulated.
256 devices in a mesh: ctx: 32 (over z, y_hi, core), head: 8 (over x, y_lo).
Axes of the slice: x: 4, y: 4 (y_hi: 2, y_lo: 2; y = y_hi * 2 + y_lo), z: 8, core: 2. Of those that a mesh axis runs over, the one named last changes fastest.
Arguments:
- queries: bfloat16 [16384, 2048], P('ctx', 'head'), may hold values from -256 to 256
- rotated_key_rows: bfloat16 [16384, 1024], P('ctx', 'head'), may hold values from -8 to 8
- value_head_rows: bfloat16 [16384, 1024], P('ctx', 'head'), may hold values from -24 to 24
- stride_offset: int32 [16], P('head'), may hold values from 0 to 7
- w_out: bfloat16 [2048, 4096], P('head'), may hold values from -0.125 to 0.125
- grad_out: bfloat16 [16384, 4096], P('ctx', 'head'), may hold values from -6 to 6
Outputs:
- layer_out: bfloat16 [16384, 4096], P('ctx', 'head')
- grad_queries: bfloat16 [16384, 2048], P('ctx', 'head')
- key_gradient: bfloat16 [16384, 1024], P('ctx', 'head')
- value_gradient: bfloat16 [16384, 1024], P('ctx', 'head')
- grad_w_out: bfloat16 [2048, 4096], P('head', 'ctx')
All inputs are finite; a program needn't handle non-finite values.
Results may differ from a plain program's by a relative error of at most 0.033.
Values may be sent and summed in bfloat16 or wider, within the bound.
A program may use at most 128 MiB of HBM per device.

v0:
```python
import math

import jax
import jax.numpy as jnp
from jax import lax
from jax.sharding import PartitionSpec as P

HEAD_SIZE = 128
BLOCK_TOKENS = 64
LOCAL = 16
STRIDE = 8


def contract_rows(form, left, right):
    return jnp.einsum(form, left, right, preferred_element_type=jnp.float32)


def exact_map(form, left, right):
    return jnp.einsum(form, left, right, precision=lax.Precision.HIGHEST)


def band_allowed(shard_id, tok_rows, phase_list):
    tokens_q = shard_id * tok_rows + jnp.arange(tok_rows, dtype=jnp.int32)
    tokens_k = (shard_id - 2) * tok_rows + jnp.arange(3 * tok_rows, dtype=jnp.int32)
    block_q = tokens_q // BLOCK_TOKENS
    block_k = tokens_k // BLOCK_TOKENS
    causal = (tokens_k[None, :] >= 0) & (tokens_k[None, :] <= tokens_q[:, None])
    nearby = block_q[:, None] - block_k[None, :] < LOCAL
    on_stride = (block_k[None, None, :] + phase_list[:, :, None]) % STRIDE == STRIDE - 1
    return causal[None, None] & (nearby[None, None] | on_stride[:, :, None, :])


def keep_state(running):
    return running


def body(queries, rotated_key_rows, value_head_rows, stride_offset, w_out, grad_out):
    tok_rows = queries.shape[0]
    groups = rotated_key_rows.shape[1] // HEAD_SIZE
    per_group = queries.shape[1] // (groups * HEAD_SIZE)
    shards = lax.axis_size("ctx")
    shard_id = lax.axis_index("ctx")
    scaling = HEAD_SIZE ** (-0.5)
    picked_rows = tok_rows // STRIDE
    picked_count = picked_rows * shards
    tile_rows = BLOCK_TOKENS * math.gcd(picked_count // BLOCK_TOKENS, max(1, 512 // BLOCK_TOKENS))
    tile_count = picked_count // tile_rows
    bound_rows = (shard_id - 2) * picked_rows
    q_heads = queries.reshape(tok_rows, groups, per_group, HEAD_SIZE)
    phase_list = stride_offset.reshape(groups, per_group)
    offsets = jnp.arange(STRIDE, dtype=jnp.int32)
    select_mask = offsets[None, None, :] == (STRIDE - 1 - phase_list)[:, :, None]

    def pick_rows(source):
        grouped = source.reshape(-1, STRIDE, BLOCK_TOKENS, groups, HEAD_SIZE)
        chosen = contract_rows("grs,nsbgd->grnbd", select_mask.astype(jnp.bfloat16), grouped)
        return chosen.astype(jnp.bfloat16)

    whole_k, whole_v = (
        lax.all_gather(rotated_key_rows, "ctx", axis=0, tiled=True),
        lax.all_gather(value_head_rows, "ctx", axis=0, tiled=True),
    )
    filler_value = jnp.zeros((2 * tok_rows, whole_k.shape[1]), jnp.bfloat16)
    near_k = lax.dynamic_slice_in_dim(
        jnp.concatenate([filler_value, whole_k], axis=0), shard_id * tok_rows, 3 * tok_rows, 0
    )
    near_v = lax.dynamic_slice_in_dim(
        jnp.concatenate([filler_value, whole_v], axis=0), shard_id * tok_rows, 3 * tok_rows, 0
    )
    picked_k = pick_rows(whole_k)
    picked_v = pick_rows(whole_v)
    near_k = near_k.reshape(3 * tok_rows, groups, HEAD_SIZE)
    near_v = near_v.reshape(3 * tok_rows, groups, HEAD_SIZE)
    picked_k = picked_k.reshape(groups, per_group, picked_count, HEAD_SIZE)
    picked_v = picked_v.reshape(groups, per_group, picked_count, HEAD_SIZE)
    allowed = band_allowed(shard_id, tok_rows, phase_list)
    scores = jnp.where(
        allowed, contract_rows("tgrd,ugd->grtu", q_heads, near_k) * scaling, -jnp.inf
    )
    row_max = jnp.max(scores, axis=-1)
    weights = jnp.where(allowed, jnp.exp(scores - row_max[..., None]), 0.0)
    row_sum = jnp.sum(weights, axis=-1)
    weighted = contract_rows("grtu,ugd->grtd", weights.astype(jnp.bfloat16), near_v)

    def forward_tile(tile_index, running):
        tile_start = tile_index * tile_rows

        def forward_update(running):
            row_max, row_sum, weighted = running
            tile_k = lax.dynamic_slice_in_dim(picked_k, tile_start, tile_rows, 2)
            tile_v = lax.dynamic_slice_in_dim(picked_v, tile_start, tile_rows, 2)
            usable = tile_start + jnp.arange(tile_rows, dtype=jnp.int32) < bound_rows
            scores = jnp.where(
                usable, contract_rows("tgrd,grkd->grtk", q_heads, tile_k) * scaling, -jnp.inf
            )
            new_max = jnp.maximum(row_max, jnp.max(scores, axis=-1))
            weights = jnp.where(usable, jnp.exp(scores - new_max[..., None]), 0.0)
            factor = jnp.exp(row_max - new_max)
            row_sum = row_sum * factor + jnp.sum(weights, axis=-1)
            weighted = weighted * factor[..., None] + contract_rows(
                "grtk,grkd->grtd", weights.astype(jnp.bfloat16), tile_v
            )
            return (new_max, row_sum, weighted)

        return lax.cond(tile_start < bound_rows, forward_update, keep_state, running)

    row_max, row_sum, weighted = lax.fori_loop(
        0, tile_count, forward_tile, (row_max, row_sum, weighted)
    )
    attended_rows = jnp.transpose(weighted / row_sum[..., None], (2, 0, 1, 3)).astype(jnp.bfloat16)
    log_total = row_max + jnp.log(row_sum)
    flat_out = attended_rows.reshape(tok_rows, -1)
    head_part = jnp.dot(flat_out, w_out, preferred_element_type=jnp.float32)
    layer_out = lax.psum_scatter(
        head_part.astype(jnp.bfloat16), "head", scatter_dimension=1, tiled=True
    )
    full_grad = lax.all_gather(grad_out, "head", axis=1, tiled=True)
    grad_flat = contract_rows("te,he->th", full_grad, w_out).astype(jnp.bfloat16)
    weight_term = contract_rows("th,te->he", flat_out, full_grad)
    grad_w_out = lax.psum_scatter(
        weight_term.astype(jnp.bfloat16), "ctx", scatter_dimension=1, tiled=True
    )
    do_heads = grad_flat.reshape(tok_rows, groups, per_group, HEAD_SIZE)
    row_dot = jnp.transpose(
        jnp.sum(do_heads.astype(jnp.float32) * attended_rows.astype(jnp.float32), axis=-1),
        (1, 2, 0),
    )
    scores = contract_rows("tgrd,ugd->grtu", q_heads, near_k) * scaling
    weights = jnp.where(allowed, jnp.exp(scores - log_total[..., None]), 0.0)
    grad_near_v = contract_rows("grtu,tgrd->ugd", weights.astype(jnp.bfloat16), do_heads)
    grad_weights = contract_rows("tgrd,ugd->grtu", do_heads, near_v)
    grad_scores = (weights * (grad_weights - row_dot[..., None])).astype(jnp.bfloat16)
    grad_q = contract_rows("grtu,ugd->tgrd", grad_scores, near_k) * scaling
    grad_near_k = contract_rows("grtu,tgrd->ugd", grad_scores, q_heads) * scaling

    def backward_tile(tile_index, inner):
        tile_start = tile_index * tile_rows

        def backward_update(inner):
            grad_q, grad_pk, grad_pv = inner
            tile_k = lax.dynamic_slice_in_dim(picked_k, tile_start, tile_rows, 2)
            tile_v = lax.dynamic_slice_in_dim(picked_v, tile_start, tile_rows, 2)
            usable = tile_start + jnp.arange(tile_rows, dtype=jnp.int32) < bound_rows
            scores = contract_rows("tgrd,grkd->grtk", q_heads, tile_k) * scaling
            weights = jnp.where(usable, jnp.exp(scores - log_total[..., None]), 0.0)
            tile_gv = contract_rows("grtk,tgrd->grkd", weights.astype(jnp.bfloat16), do_heads)
            grad_weights = contract_rows("tgrd,grkd->grtk", do_heads, tile_v)
            grad_scores = (weights * (grad_weights - row_dot[..., None])).astype(jnp.bfloat16)
            grad_q = grad_q + contract_rows("grtk,grkd->tgrd", grad_scores, tile_k) * scaling
            tile_gk = contract_rows("grtk,tgrd->grkd", grad_scores, q_heads) * scaling
            grad_pk = lax.dynamic_update_slice_in_dim(grad_pk, tile_gk, tile_start, 2)
            grad_pv = lax.dynamic_update_slice_in_dim(grad_pv, tile_gv, tile_start, 2)
            return (grad_q, grad_pk, grad_pv)

        return lax.cond(tile_start < bound_rows, backward_update, keep_state, inner)

    empty_state = jnp.zeros((groups, per_group, picked_count, HEAD_SIZE), jnp.float32)
    grad_q, grad_pk, grad_pv = lax.fori_loop(
        0, tile_count, backward_tile, (grad_q, empty_state, empty_state)
    )
    grad_queries = grad_q.astype(jnp.bfloat16).reshape(tok_rows, -1)

    def place(picked_gradient, grad_near):
        spread_row_list = exact_map(
            "xij,xiucz->ujcxz",
            select_mask.astype(jnp.float32),
            picked_gradient.reshape(groups, per_group, -1, BLOCK_TOKENS, HEAD_SIZE),
        )
        spread_row_list = spread_row_list.reshape(picked_count * STRIDE, groups, HEAD_SIZE)
        padded = jnp.concatenate(
            [jnp.zeros((2 * tok_rows, groups, HEAD_SIZE), jnp.float32), spread_row_list], axis=0
        )
        region = lax.dynamic_slice_in_dim(padded, shard_id * tok_rows, 3 * tok_rows, 0) + grad_near
        padded = lax.dynamic_update_slice_in_dim(padded, region, shard_id * tok_rows, 0)
        return padded[2 * tok_rows :]

    own_k, own_v = (
        lax.psum_scatter(
            place(grad_pk, grad_near_k).astype(jnp.bfloat16), "ctx", scatter_dimension=0, tiled=True
        ).astype(jnp.float32),
        lax.psum_scatter(
            place(grad_pv, grad_near_v).astype(jnp.bfloat16), "ctx", scatter_dimension=0, tiled=True
        ).astype(jnp.float32),
    )
    key_gradient = own_k.astype(jnp.bfloat16).reshape(tok_rows, groups * HEAD_SIZE)
    value_gradient = own_v.astype(jnp.bfloat16).reshape(tok_rows, groups * HEAD_SIZE)
    return (layer_out, grad_queries, key_gradient, value_gradient, grad_w_out)


def solution(mesh):
    placed = (
        P("ctx", "head"),
        P("ctx", "head"),
        P("ctx", "head"),
        P("head"),
        P("head", None),
        P("ctx", "head"),
    )
    return jax.shard_map(
        body,
        mesh=mesh,
        in_specs=placed,
        out_specs=(
            P("ctx", "head"),
            P("ctx", "head"),
            P("ctx", "head"),
            P("ctx", "head"),
            P("head", "ctx"),
        ),
        check_vma=False,
    )
```

profile of v0, /device:TPU:14, one launch (start us, length us, event | category | flops | bytes accessed | tf_op | source)
XLA Modules:
  0.0 814.1 jit_solution(18127098007945451862)
XLA Ops:
  15.5 88.2 %all-gather.8.cloned.1.call-done = bf16[512,4096]{1,0:T(8,128)(2,1)} async-done(((bf16[512,512]{1,0:T(8,128)(2,1)}), bf16[512,4096]{1,0:T(8,128)(2,1)}) %all-gather.8.cloned.1.call-update) | async-done | bytes 4194320 | tf_op jit(solution)/shard_map/all_gather | solution.py:117
  103.7 4.2 convolution_convert_fusion.2
  107.9 86.4 %all-gather.6.cloned.1.call-done = bf16[16384,128]{1,0:T(8,128)(2,1)} async-done(((bf16[512,128]{1,0:T(8,128)(2,1)}), bf16[16384,128]{1,0:T(8,128)(2,1)}) %all-gather.6.cloned.1.call-update) | async-done | bytes 4194320 | tf_op jit(solution)/shard_map/all_gather | solution.py:61
  194.3 5.0 fusion.81
  200.5 79.9 %all-gather.4.cloned.1.call-done = bf16[16384,128]{1,0:T(8,128)(2,1)} async-done(((bf16[512,128]{1,0:T(8,128)(2,1)}), bf16[16384,128]{1,0:T(8,128)(2,1)}) %all-gather.4.cloned.1.call-update) | async-done | bytes 4194320 | tf_op jit(solution)/shard_map/all_gather | solution.py:60
  280.4 5.1 fusion.78
  288.0 15.1 %fusion.62 = f32[2,512]{1,0:T(2,128)S(1)} fusion(f32[2,512]{1,0:T(2,128)S(1)} %get-tuple-element.541, f32[1536,512,2]{1,0,2:T(8,128)S(1)} %get-tuple-element.542, pred[2,1536]{1,0:T(4,128)(4,1)S(1)} %fusion.98, pred[512,1536]{0,1:T(8,128)(4,1)S(1)} %copy-done.8, pred[512,1536]{0,1:T(8,128)(4,1)S(1)} %copy-done.10), kind=kLoop, calls=%fused_computation.88 | loop fusion | flops 11009024 | bytes 7875584 | tf_op jit(solution)/shard_map/reduce_sum | solution.py:82
  303.2 3.8 fusion.85
  307.0 2.4 copy.69
  311.3 4.8 convolution_convert_fusion.1
  316.2 4.1 copy.96
  321.5 5.3 fusion.52
  331.5 6.8 convolution_bitcast_fusion.2
  338.3 4.9 copy.82
  343.2 9.1 %copy.83 = f32[16384,1,128]{0,2,1:T(8,128)} copy(f32[16384,1,128]{2,0,1:T(8,128)} %bitcast.255) | data formatting | bytes 16777216 | tf_op jit(solution)/shard_map/reshape | solution.py:169
  352.3 4.6 concatenate.15
  356.9 5.2 fusion.71
  362.1 2.4 slice.14
  364.6 6.8 convolution_bitcast_fusion.3
  379.1 3.3 convolution_convert_fusion
  383.3 68.5 %reduce-scatter.13.cloned.1.call-done = bf16[128,256]{1,0:T(8,128)(2,1)} async-done(((bf16[4096,256]{1,0:T(8,128)(2,1)}), bf16[128,256]{1,0:T(8,128)(2,1)}) %reduce-scatter.13.cloned.1.call-update) | async-done | bytes 65552
  453.4 128.9 %reduce-scatter.11.cloned.1.call-done = bf16[512,1,128]{0,2,1:T(8,128)(2,1)} async-done(((bf16[16384,1,128]{0,2,1:T(8,128)(2,1)}), bf16[512,1,128]{0,2,1:T(8,128)(2,1)}) %reduce-scatter.11.cloned.1.call-update) | async-done | bytes 131088 | tf_op jit(solution)/shard_map/reduce_scatter | solution.py:181
  584.0 129.3 %reduce-scatter.9.cloned.1.call-done = bf16[512,1,128]{2,0,1:T(8,128)(2,1)} async-done(((bf16[16384,1,128]{2,0,1:T(8,128)(2,1)}), bf16[512,1,128]{2,0,1:T(8,128)(2,1)}) %reduce-scatter.9.cloned.1.call-update) | async-done | bytes 131088 | tf_op jit(solution)/shard_map/reduce_scatter | solution.py:178
  713.2 93.6 %reduce-scatter.7.cloned.1.call-done = bf16[512,512]{1,0:T(8,128)(2,1)} async-done(((bf16[512,4096]{1,0:T(8,128)(2,1)}), bf16[512,512]{1,0:T(8,128)(2,1)}) %reduce-scatter.7.cloned.1.call-update) | async-done | bytes 524304 | tf_op jit(solution)/shard_map/reduce_scatter | solution.py:114
  (84 shorter events, 31.5 us)
Async XLA Ops:
  7.2 96.6 %copy-start = (bf16[256,4096]{1,0:T(8,128)(2,1)S(1)}, bf16[256,4096]{1,0:T(8,128)(2,1)}, u32[]{:S(2)}) copy-start(bf16[256,4096]{1,0:T(8,128)(2,1)} %param.18) | copy-start | bytes 6291460
  7.2 96.5 %all-gather.8.cloned.1.call-start = ((), (), s32[]{:S(2)}) async-start(), calls=%async_computation.7 | async-start | bytes 4718592 | tf_op jit(solution)/shard_map/all_gather | solution.py:117
  7.9 186.4 %all-gather.6.cloned.1.call-start = ((), (), s32[]{:S(2)}) async-start(), calls=%async_computation.5 | async-start | bytes 4325376 | tf_op jit(solution)/shard_map/all_gather | solution.py:61
  8.7 271.8 %all-gather.4.cloned.1.call-start = ((), (), s32[]{:S(2)}) async-start(), calls=%async_computation.4 | async-start | bytes 4325376 | tf_op jit(solution)/shard_map/all_gather | solution.py:60
  9.4 442.4 %reduce-scatter.13.cloned.1.call-start = ((), (), s32[]{:S(2)}) async-start(), calls=%async_computation.10 | async-start | bytes 2162688
  280.4 5.3 copy-start.3
  280.4 5.3 copy-start.8
  280.4 5.3 copy-start.10
  280.4 5.3 copy-start.12
  288.0 15.2 %copy-start.6 = (f32[1536,512,2]{1,0,2:T(8,128)}, f32[1536,512,2]{1,0,2:T(8,128)S(1)}, u32[]{:S(2)}) copy-start(f32[1536,512,2]{1,0,2:T(8,128)S(1)} %get-tuple-element.542) | copy-start | bytes 18874372
  288.0 15.2 %copy-start.7 = (bf16[16384,128]{1,0:T(8,128)(2,1)S(1)}, bf16[16384,128]{1,0:T(8,128)(2,1)}, u32[]{:S(2)}) copy-start(bf16[16384,128]{1,0:T(8,128)(2,1)} %all-gather.6.cloned.1.call-done) | copy-start | bytes 12582916
  307.0 9.2 %copy-start.5 = (bf16[1,2,2048,128]{3,2,1,0:T(8,128)(2,1)}, bf16[1,2,2048,128]{3,2,1,0:T(8,128)(2,1)S(1)}, u32[]{:S(2)}) copy-start(bf16[1,2,2048,128]{3,2,1,0:T(8,128)(2,1)S(1)} %get-tuple-element.774) | copy-start | bytes 3145732
  310.6 0.7 copy-start.14
  320.3 262.0 %reduce-scatter.11.cloned.1.call-start = ((), (), s32[]{:S(2)}) async-start(), calls=%async_computation.9 | async-start | bytes 4325376 | tf_op jit(solution)/shard_map/reduce_scatter | solution.py:181
  321.4 5.3 copy-start.4
  326.8 1.7 copy-start.1
  352.3 4.6 copy-start.9
  352.3 4.6 copy-start.11
  352.3 4.6 copy-start.16
  364.6 348.7 %reduce-scatter.9.cloned.1.call-start = ((), (), s32[]{:S(2)}) async-start(), calls=%async_computation.8 | async-start | bytes 4325376 | tf_op jit(solution)/shard_map/reduce_scatter | solution.py:178
  373.0 1.9 copy-start.2
  373.1 1.9 copy-start.13
  378.1 0.9 copy-start.15
  378.2 428.7 %reduce-scatter.7.cloned.1.call-start = ((), (), s32[]{:S(2)}) async-start(), calls=%async_computation.6 | async-start | bytes 4718592 | tf_op jit(solution)/shard_map/reduce_scatter | solution.py:114
Sparse Core Ops, SparseCore 0:
  9.8 93.8 all-gather.7
  106.5 87.7 all-gather.5
  197.1 83.2 all-gather.3
  320.4 131.3 reduce-scatter.12
  455.9 126.3 reduce-scatter.10
  587.0 126.2 reduce-scatter.8
  716.4 90.4 reduce-scatter.6
where the time goes:
time: 826 us; the launch traced here: 814 us
  waiting for transfers between devices  677 us (82%)
  matrix products  54.4 us (7%)
  local copies, waits for them, and re-layouts  46.4 us (6%)
  other arithmetic  21.2 us (3%)
  between operations  14.8 us (2%)
    reduce_scatter x1, waiting for transfers between devices, body(): lax.psum_scatter(place(grad_pk, grad_near_k).astype(jnp.bfloat16), 'ctx',...  129 us
    reduce_scatter x1, waiting for transfers between devices, body(): lax.psum_scatter(place(grad_pv, grad_near_v).astype(jnp.bfloat16), 'ctx',...  129 us
    reduce_scatter x1, waiting for transfers between devices, body(): lax.psum_scatter(head_part.astype(jnp.bfloat16), 'head', scatter_dimensio...  93.6 us
    all_gather x1, waiting for transfers between devices, body(): full_grad = lax.all_gather(grad_out, 'head', axis=1, tiled=True)  88.2 us
    all_gather x1, waiting for transfers between devices, body(): lax.all_gather(value_head_rows, 'ctx', axis=0, tiled=True)  86.4 us
    all_gather x1, waiting for transfers between devices, body(): lax.all_gather(rotated_key_rows, 'ctx', axis=0, tiled=True)  79.9 us
    unnamed x8, waiting for transfers between devices  70.6 us
    dot_general x10, matrix products, contract_rows(): return jnp.einsum(form, left, right, preferred_element_type=jnp.float32)  37.6 us
  transfers between devices with their start and end apart: 7, of which 7 were waited for; matrix products, arithmetic and copies ran while one was open for 10% of the time, Pallas kernels for 0%

commit v1 on v0

v1 whole, which is shorter than its diff:
```python
import jax
import jax.numpy as jnp
from jax import lax
from jax.experimental import pallas as pl
from jax.experimental.pallas import tpu as pltpu
from jax.sharding import PartitionSpec as P

T = 512
DH = 128
BLK = 64
NH = 8
NC = 32
SCALE = DH ** -0.5
EXP2_SCALE = SCALE * 1.4426950408889634
NEG = -1e30
MESH = pl.DeviceIdType.MESH
BF = jnp.bfloat16
F32 = jnp.float32


def where_am_i():
    c = lax.axis_index("ctx")
    h = lax.axis_index("head")
    return c, h, c // 4, (c // 2) % 2, c % 2


def ctx_id(z, yh, core):
    return z * 4 + yh * 2 + core


def signal(barrier, c, h):
    pl.semaphore_signal(barrier, inc=1, device_id=(c, h), device_id_type=MESH)


class Sends:
    def __init__(self, sems):
        self.sems, self.made = sems, []

    def start(self, src, dst, recv, c, h):
        copy = pltpu.make_async_remote_copy(
            src_ref=src, dst_ref=dst, send_sem=self.sems.at[len(self.made)],
            recv_sem=recv, device_id=(c, h), device_id_type=MESH)
        copy.start()
        self.made.append(copy)

    def finish(self):
        for copy in self.made:
            copy.wait_send()


def arrived(ref, recv, send, c, h):
    pltpu.make_async_remote_copy(
        src_ref=ref, dst_ref=ref, send_sem=send, recv_sem=recv,
        device_id=(c, h), device_id_type=MESH).wait_recv()


def gather_kernel(off_ref, k_ref, v_ref, w_ref, picked, near, wc,
                  send, pk_recv, w_recv, c_recv, b_recv, local):
    c, h, z, yh, core = where_am_i()
    partner = c + 1 - 2 * core
    ypeer = ctx_id(z, 1 - yh, core)
    after, before = lax.rem(c + 2, NC), lax.rem(c + NC - 2, NC)
    barrier = pltpu.get_barrier_semaphore()
    zs = [ctx_id(lax.rem(z + d, 8), yh, core) for d in (1, 7, 2, 6, 3, 5, 4)]
    zys = [ctx_id(lax.rem(z + d, 8), 1 - yh, core) for d in (1, 7, 2, 6, 3, 5, 4)]
    hs = [lax.rem(h + d, NH) for d in range(1, NH)]
    for peer in [partner, ypeer, after, before] + zs:
        signal(barrier, peer, h)
    for peer in hs:
        signal(barrier, c, peer)
    for r in range(2):
        wanted = jnp.full((BLK, DH), 7 - off_ref[r], jnp.int32)
        for source, slot in ((k_ref, r), (v_ref, 2 + r)):
            rows = source[:BLK].astype(F32)
            for b in range(1, 8):
                rows = jnp.where(wanted == b, source[b * BLK:(b + 1) * BLK].astype(F32), rows)
            picked[slot, c] = rows.astype(BF)
    copies = [
        pltpu.make_async_copy(k_ref, near.at[0, 0], local.at[0]),
        pltpu.make_async_copy(v_ref, near.at[1, 0], local.at[1]),
        pltpu.make_async_copy(
            w_ref.at[:, pl.ds(pl.multiple_of(h * T, T), T)],
            wc.at[pl.ds(pl.multiple_of(h * 256, 256), 256), :], local.at[2]),
    ]
    for copy in copies:
        copy.start()
    pl.semaphore_wait(barrier, 4 + 7 + 7)

    sends = Sends(send)

    def block(t):
        return picked.at[:, t]

    def piece(half, r):
        return wc.at[pl.ds(pl.multiple_of(r * 256, 256), 256),
                     pl.ds(pl.multiple_of(half * 256, 256), 256)]

    sends.start(block(c), block(c), pk_recv.at[c], ypeer, h)
    sends.start(k_ref, near.at[0, 2], c_recv.at[0], after, h)
    sends.start(v_ref, near.at[1, 2], c_recv.at[1], after, h)
    for n in range(7):
        sends.start(block(c), block(c), pk_recv.at[c], zs[n], h)
        sends.start(
            w_ref.at[:, pl.ds(pl.multiple_of(hs[n] * T + core * 256, 256), 256)],
            piece(core, h), w_recv.at[core, h], c, hs[n])
    sends.start(block(c), block(c), pk_recv.at[c], partner, h)

    arrived(block(ypeer), pk_recv.at[ypeer], send.at[0], ypeer, h)
    for n in range(7):
        sends.start(block(ypeer), block(ypeer), pk_recv.at[ypeer], zs[n], h)
    sends.start(block(ypeer), block(ypeer), pk_recv.at[ypeer], partner, h)

    arrived(near.at[0, 2], c_recv.at[0], send.at[0], before, h)
    arrived(near.at[1, 2], c_recv.at[1], send.at[0], before, h)
    for copy in copies:
        copy.wait()
    give = 2 * core
    sends.start(near.at[0, give], near.at[0, 1], b_recv.at[0], partner, h)
    sends.start(near.at[1, give], near.at[1, 1], b_recv.at[1], partner, h)
    for n in range(7):
        arrived(piece(core, hs[n]), w_recv.at[core, hs[n]], send.at[0], c, hs[n])
        sends.start(piece(core, hs[n]), piece(core, hs[n]), w_recv.at[core, hs[n]], partner, h)
        arrived(block(zs[n]), pk_recv.at[zs[n]], send.at[0], zs[n], h)
        sends.start(block(zs[n]), block(zs[n]), pk_recv.at[zs[n]], partner, h)
    for n in range(7):
        arrived(block(zys[n]), pk_recv.at[zys[n]], send.at[0], zs[n], h)
        sends.start(block(zys[n]), block(zys[n]), pk_recv.at[zys[n]], partner, h)
    flip = 1 - 2 * core
    for t in [c, ypeer] + zs + zys:
        arrived(block(t + flip), pk_recv.at[t + flip], send.at[0], partner, h)
    for n in range(7):
        arrived(piece(1 - core, hs[n]), w_recv.at[1 - core, hs[n]], send.at[0], partner, h)
    arrived(near.at[0, 1], b_recv.at[0], send.at[0], partner, h)
    arrived(near.at[1, 1], b_recv.at[1], send.at[0], partner, h)
    sends.finish()


def fold(x, op):
    return op(x.reshape(T // 8, 8, T), axis=0)


def nt(a, b):
    return lax.dot_general(a, b, (((1,), (1,)), ((), ())), preferred_element_type=F32)


def tn(a, b):
    return lax.dot_general(a, b, (((0,), (0,)), ((), ())), preferred_element_type=F32)


def nn(a, b):
    return jnp.dot(a, b, preferred_element_type=F32)


def attention_kernel(off_ref, q_ref, near, picked, gpart,
                     att_all, gq_ref, gnear, gpick,
                     qs, scores, probs, grecv, dnear, top, inv, acc, dog,
                     send, g_recv, a_recv):
    c, h, z, yh, core = where_am_i()
    barrier = pltpu.get_barrier_semaphore()
    hs = [lax.rem(h + d, NH) for d in range(1, NH)]
    for peer in hs:
        signal(barrier, c, peer)
    for r in range(2):
        qs[r] = q_ref[:, r * DH:(r + 1) * DH]
    dnear[...] = jnp.zeros_like(dnear)
    pl.semaphore_wait(barrier, 7)
    sends = Sends(send)
    for peer in hs:
        sends.start(gpart.at[peer], grecv.at[h], g_recv.at[h], c, peer)

    def tile(p):
        return pl.ds(pl.multiple_of(p * 8, 8), 8)

    def forward(r, _):
        q = qs[r]
        key = lax.broadcasted_iota(jnp.int32, (T, T), 0)
        query = lax.broadcasted_iota(jnp.int32, (T, T), 1)
        s = jnp.where(key <= query, nt(near[0, 0], q), NEG)
        scores[0] = s
        top[...] = fold(s, jnp.max)
        s = jnp.where(c >= 1, nt(near[0, 1], q), NEG)
        scores[1] = s
        top[...] = jnp.maximum(top[...], fold(s, jnp.max))
        kb, qb = key // BLK, query // BLK
        ok = ((kb > qb) | (kb == 7 - off_ref[r])) & (c >= 2)
        s = jnp.where(ok, nt(near[0, 2], q), NEG)
        scores[2] = s
        top[...] = jnp.maximum(top[...], fold(s, jnp.max))

        def pick_scores(p, _):
            rows = lax.broadcasted_iota(jnp.int32, (T, T), 0)
            s = nt(picked[r, tile(p)].reshape(T, DH), q)
            s = jnp.where(rows < (c - 2) * BLK - p * T, s, NEG)
            scores[3 + p] = s
            top[...] = jnp.maximum(top[...], fold(s, jnp.max))
            return 0

        lax.fori_loop(0, 4, pick_scores, 0)
        m = jnp.max(top[...], axis=0, keepdims=True)
        top[...] = jnp.zeros_like(top)
        acc[...] = jnp.zeros_like(acc)

        def weigh(i, values):
            w = jnp.exp2((scores[i] - m) * EXP2_SCALE)
            top[...] += fold(w, jnp.sum)
            w = w.astype(BF)
            probs[r, i] = w
            acc[...] += tn(values, w)

        def near_mix(i, _):
            weigh(i, near[1, i])
            return 0

        def pick_mix(p, _):
            weigh(3 + p, picked[2 + r, tile(p)].reshape(T, DH))
            return 0

        lax.fori_loop(0, 3, near_mix, 0)
        lax.fori_loop(0, 4, pick_mix, 0)
        total = 1.0 / jnp.sum(top[...], axis=0, keepdims=True)
        inv[r] = jnp.broadcast_to(total, (8, T))
        att_all[h, pl.ds(pl.multiple_of(r * DH, DH), DH), :] = (acc[...] * total).astype(BF)
        return 0

    lax.fori_loop(0, 2, forward, 0)
    for peer in hs:
        sends.start(att_all.at[h], att_all.at[h], a_recv.at[h], c, peer)
    for peer in hs:
        arrived(grecv.at[peer], g_recv.at[peer], send.at[0], c, peer)

    def backward(r, _):
        rows = pl.ds(pl.multiple_of(r * DH, DH), DH)
        grad = gpart[h, rows, :].astype(F32)
        for peer in hs:
            grad += grecv[peer, rows, :].astype(F32)
        grad = grad.astype(BF).astype(F32)
        total = inv[r, 0:1]
        rowdot = jnp.sum(grad * att_all[h, rows, :].astype(F32), axis=0, keepdims=True) * total
        dog[...] = (grad * total).T.astype(BF)
        acc[...] = jnp.zeros_like(acc)

        def grads(i, keys, values):
            w = probs[r, i]
            do = dog[...]
            dp = nt(values, do)
            ds = (w.astype(F32) * (dp - rowdot)).astype(BF)
            acc[...] += tn(keys, ds)
            return nn(ds, qs[r]) * SCALE, nn(w, do)

        def near_grads(i, _):
            dk, dv = grads(i, near[0, i], near[1, i])
            dnear[0, i] += dk
            dnear[1, i] += dv
            return 0

        def pick_grads(p, _):
            dk, dv = grads(3 + p, picked[r, tile(p)].reshape(T, DH),
                           picked[2 + r, tile(p)].reshape(T, DH))
            gpick[r, tile(p)] = dk.astype(BF).reshape(8, BLK, DH)
            gpick[2 + r, tile(p)] = dv.astype(BF).reshape(8, BLK, DH)
            return 0

        lax.fori_loop(0, 3, near_grads, 0)
        lax.fori_loop(0, 4, pick_grads, 0)
        qs[r] = (acc[...].T * SCALE).astype(BF)
        return 0

    lax.fori_loop(0, 2, backward, 0)
    for r in range(2):
        gq_ref[:, r * DH:(r + 1) * DH] = qs[r]
    gnear[...] = dnear[...].astype(BF)
    for peer in hs:
        arrived(att_all.at[peer], a_recv.at[peer], send.at[0], c, peer)
    sends.finish()


def scatter_kernel(off_ref, wt, gpick, gnear, gk_ref, gv_ref, gw_ref,
                   wrecv, wsum, wslot, precv, psum, pslot, brecv, csum, crecv,
                   send, pair_recv, w_recv, p_recv, c_recv, local):
    c, h, z, yh, core = where_am_i()
    partner = c + 1 - 2 * core
    after, before = lax.rem(c + 2, NC), lax.rem(c + NC - 2, NC)
    barrier = pltpu.get_barrier_semaphore()
    places = [(d, y) for d in (4, 3, 5, 2, 6, 1, 7, 0) for y in (1, 0)]
    ids = []
    for d, y in places:
        zz = lax.rem(z + d, 8)
        yy = lax.rem(yh + y, 2)
        ids.append((zz, yy, ctx_id(zz, yy, core)))
    me = z * 2 + yh

    def dest(n):
        r = lax.rem(h + places[n][0], NH)
        y = lax.rem(yh + places[n][1], 2)
        return r, y, ctx_id(h, y, core)

    signal(barrier, partner, h)
    signal(barrier, after, h)
    signal(barrier, before, h)
    for n in range(15):
        signal(barrier, ids[n][2], h)
    for n in range(16):
        r, y, t = dest(n)

        @pl.when((t != c) | (r != h))
        def _():
            signal(barrier, t, r)

        source = ids[n][2]

        @pl.when((source != c) | (z != h))
        def _():
            signal(barrier, source, z)

    pl.semaphore_wait(barrier, jnp.where(z == h, 18 + 30, 18 + 32))

    sends = Sends(send)
    sends.start(gnear.at[:, 1], brecv, pair_recv.at[0], partner, h)
    sends.start(gpick.at[:, :, 1 - core], precv, pair_recv.at[1], partner, h)
    for y in range(2):
        sends.start(wt.at[:, pl.ds(pl.multiple_of((2 * y + 1 - core) * DH, DH), DH)],
                    wrecv.at[y], pair_recv.at[2 + y], partner, h)

    arrived(brecv, pair_recv.at[0], send.at[0], partner, h)
    extra = brecv[...].astype(F32)
    isodd = (core == 1)
    csum[...] = (gnear[:, 2].astype(F32) + jnp.where(isodd, extra, 0.0)).astype(BF)
    arrived(precv, pair_recv.at[1], send.at[0], partner, h)

    def pick_sum(n, _):
        psum[:, n] = (gpick[:, n, core].astype(F32) + precv[:, n].astype(F32)).astype(BF)
        return 0

    lax.fori_loop(0, 16, pick_sum, 0)
    sends.start(csum, crecv, c_recv.at[0], before, h)
    for n in range(15):
        zz, yy, t = ids[n]
        sends.start(psum.at[:, zz * 2 + yy], pslot.at[me], p_recv.at[me], t, h)

    for y in range(2):
        arrived(wrecv.at[y], pair_recv.at[2 + y], send.at[0], partner, h)
        mine = wt[:, pl.ds(pl.multiple_of((2 * y + core) * DH, DH), DH)]
        wsum[y] = (mine.astype(F32) + wrecv[y].astype(F32)).astype(BF)
    base = len(sends.made)

    def w_copy(n):
        r, y, t = dest(n)
        rows = pl.ds(pl.multiple_of(r * 256, 256), 256)
        return (r, t), wsum.at[y, rows, :], pltpu.make_async_remote_copy(
            src_ref=wsum.at[y, rows, :], dst_ref=wslot.at[me],
            send_sem=send.at[base + n], recv_sem=w_recv.at[me],
            device_id=(t, r), device_id_type=MESH)

    for n in range(16):
        (r, t), src, copy = w_copy(n)

        @pl.when((t != c) | (r != h))
        def _():
            copy.start()

        @pl.when((t == c) & (r == h))
        def _():
            own = pltpu.make_async_copy(src, wslot.at[me], local)
            own.start()
            own.wait()

    arrived(crecv, c_recv.at[0], send.at[0], after, h)
    grad = gnear[:, 0].astype(F32) + jnp.where(isodd, 0.0, extra) + crecv[...].astype(F32)
    for n in range(15):
        zz, yy, t = ids[n]
        arrived(pslot.at[zz * 2 + yy], p_recv.at[zz * 2 + yy], send.at[0], t, h)
    pslot[me] = psum[:, me]
    total = pslot[0].astype(F32)
    for n in range(1, 16):
        total += pslot[n].astype(F32)
    block = lax.broadcasted_iota(jnp.int32, (T, DH), 0) // BLK
    for n, out in enumerate((gk_ref, gv_ref)):
        g = grad[n]
        for r in range(2):
            spread = jnp.concatenate([total[2 * n + r]] * 8, axis=0)
            g += jnp.where(block == 7 - off_ref[r], spread, 0.0)
        out[...] = g.astype(BF)
    for n in range(16):
        zz, yy, source = ids[n]

        @pl.when((source != c) | (z != h))
        def _():
            arrived(wslot.at[zz * 2 + yy], w_recv.at[zz * 2 + yy], send.at[0], source, z)

    total = wslot[0].astype(F32)
    for n in range(1, 16):
        total += wslot[n].astype(F32)
    gw_ref[...] = total.astype(BF)
    sends.finish()
    for n in range(16):
        (r, t), src, copy = w_copy(n)

        @pl.when((t != c) | (r != h))
        def _():
            copy.wait_send()


VM = pl.BlockSpec(memory_space=pltpu.VMEM)
SM = pl.BlockSpec(memory_space=pltpu.SMEM)
DMA = pltpu.SemaphoreType.DMA


def shaped(*shape, dtype=BF):
    return jax.ShapeDtypeStruct(shape, dtype)


def params(number):
    return pltpu.CompilerParams(
        collective_id=number, has_side_effects=True, vmem_limit_bytes=60 << 20)


def body(queries, keys, values, stride_offset, w_out, grad_out):
    picked, near, wc = pl.pallas_call(
        gather_kernel,
        out_shape=(shaped(4, NC, BLK, DH), shaped(2, 3, T, DH), shaped(2048, T)),
        in_specs=[SM, VM, VM, VM],
        out_specs=(VM, VM, VM),
        scratch_shapes=[DMA((54,)), DMA((NC,)), DMA((2, NH)), DMA((2,)), DMA((2,)), DMA((3,))],
        compiler_params=params(0),
        name="gather_rows",
    )(stride_offset, keys, values, w_out)
    gpart = lax.dot_general(wc, grad_out, (((1,), (1,)), ((), ())), preferred_element_type=F32)
    gpart = gpart.astype(BF).reshape(NH, 256, T)
    att_all, grad_queries, gnear, gpick = pl.pallas_call(
        attention_kernel,
        out_shape=(shaped(NH, 256, T), shaped(T, 256), shaped(2, 3, T, DH),
                   shaped(4, NC, BLK, DH)),
        in_specs=[SM, VM, VM, VM, VM],
        out_specs=(VM, VM, VM, VM),
        scratch_shapes=[
            pltpu.VMEM((2, T, DH), BF), pltpu.VMEM((7, T, T), F32),
            pltpu.VMEM((2, 7, T, T), BF), pltpu.VMEM((NH, 256, T), BF),
            pltpu.VMEM((2, 3, T, DH), F32), pltpu.VMEM((8, T), F32),
            pltpu.VMEM((2, 8, T), F32), pltpu.VMEM((DH, T), F32), pltpu.VMEM((T, DH), BF),
            DMA((14,)), DMA((NH,)), DMA((NH,)),
        ],
        compiler_params=params(1),
        name="attend",
    )(stride_offset, queries, near, picked, gpart)
    att = att_all.reshape(2048, T)
    layer_out = lax.dot_general(
        att, wc, (((0,), (0,)), ((), ())), preferred_element_type=F32).astype(BF)
    wt = jnp.dot(att, grad_out, preferred_element_type=F32).astype(BF)
    gk, gv, gw = pl.pallas_call(
        scatter_kernel,
        out_shape=(shaped(T, DH), shaped(T, DH), shaped(256, DH)),
        in_specs=[SM, VM, VM, VM],
        out_specs=(VM, VM, VM),
        scratch_shapes=[
            pltpu.VMEM((2, 2048, DH), BF), pltpu.VMEM((2, 2048, DH), BF),
            pltpu.VMEM((16, 256, DH), BF), pltpu.VMEM((4, 16, BLK, DH), BF),
            pltpu.VMEM((4, 16, BLK, DH), BF), pltpu.VMEM((16, 4, BLK, DH), BF),
            pltpu.VMEM((2, T, DH), BF), pltpu.VMEM((2, T, DH), BF), pltpu.VMEM((2, T, DH), BF),
            DMA((40,)), DMA((4,)), DMA((16,)), DMA((16,)), DMA((1,)), DMA,
        ],
        compiler_params=params(2),
        name="scatter_grads",
    )(stride_offset, wt, gpick.reshape(4, 16, 2, BLK, DH), gnear)
    return layer_out, grad_queries, gk, gv, gw


def solution(mesh):
    return jax.shard_map(
        body,
        mesh=mesh,
        in_specs=(P("ctx", "head"), P("ctx", "head"), P("ctx", "head"), P("head"),
                  P("head", None), P("ctx", "head")),
        out_specs=(P("ctx", "head"), P("ctx", "head"), P("ctx", "head"), P("ctx", "head"),
                   P("head", "ctx")),
        check_vma=False,
    )
```

time: 826 us -> 284 us (0.34)
  waiting for transfers between devices: 677 us -> 0 us
  Pallas kernels: 0 us -> 263 us
  matrix products: 54.4 us -> 10.6 us
  local copies, waits for them, and re-layouts: 46.4 us -> 5.33 us
  other arithmetic: 21.2 us -> 0 us
  between operations: 14.8 us -> 0.7 us
    reduce_scatter x3 -> x0, waiting for transfers between devices: 352 us -> none  [the longest x1 129 us: body(): lax.psum_scatter(place(grad_pk, grad_near_k).astype(jnp.bfloat16), 'ctx',...]
    pallas_call x0 -> x3, Pallas kernels: none -> 263 us  [the longest x1 148 us: body(): pl.pallas_call(scatter_kernel, out_shape=(shaped(T, DH), shaped(T, DH), s...]
    all_gather x3 -> x0, waiting for transfers between devices: 255 us -> none  [the longest x1 88.2 us: body(): full_grad = lax.all_gather(grad_out, 'head', axis=1, tiled=True)]
    unnamed x8 -> x0, waiting for transfers between devices: 70.6 us -> none
    dot_general x13 -> x3, matrix products: 54.4 us -> 10.6 us  [the longest x1 4.24 us: body(): lax.dot_general(wc, grad_out, (((1,), (1,)), ((), ())), preferred_element...]
    reduce_sum x2 -> x0, other arithmetic: 16.4 us -> none  [the longest x1 15.1 us: body(): row_sum = jnp.sum(weights, axis=-1)]
    reshape x2 -> x0, local copies, waits for them, and re-layouts: 9.93 us -> none  [the longest x1 9.09 us: place(): spread_row_list.reshape(picked_count * STRIDE, groups, HEAD_SIZE)]
  transfers between devices with their start and end apart: 7 -> 0, of which waited for: 7 -> 0; matrix products, arithmetic and copies ran while one was open for 10% -> 0% of each run, Pallas kernels for 0% -> 0%
where the time goes in v1:
time: 284 us; the launch traced here: 279 us
  Pallas kernels  263 us (93%)
  matrix products  10.6 us (4%)
  local copies, waits for them, and re-layouts  5.33 us (2%)
    pallas_call x1, Pallas kernels, body(): pl.pallas_call(scatter_kernel, out_shape=(shaped(T, DH), shaped(T, DH), s...  148 us
    pallas_call x1, Pallas kernels, body(): pl.pallas_call(attention_kernel, out_shape=(shaped(NH, 256, T), shaped(T,...  71.4 us
    pallas_call x1, Pallas kernels, body(): pl.pallas_call(gather_kernel, out_shape=(shaped(4, NC, BLK, DH), shaped(2...  43.2 us

profile of v1, /device:TPU:14, one launch (start us, length us, event | category | flops | bytes accessed | tf_op | source)
XLA Modules:
  0.0 279.2 jit_solution(935737757474513317)
XLA Ops:
  0.6 0.0 copy-start
  0.6 43.2 %gather_rows.1 = (bf16[4,32,64,128]{3,2,1,0:T(8,128)(2,1)}, bf16[2,3,512,128]{3,2,1,0:T(8,128)(2,1)}, bf16[2048,512]{1,0:T(8,128)(2,1)}) custom-call(s32[2]{0:T(128)} %off_ref.5, bf16[512,128]{1,0:T(8,128)(2,1)} %k_ref.1, bf16[512,128]{1,0:T(8,128)(2,1)} %v_ref.1, bf16[256,4096]{1,0:T(8,128)(2,1)} %w_ref.1), custom_call_target="tpu_custom_call" | custom-call | tf_op jit(solution)/shard_map/gather_rows/pallas_call | solution.py:418
  43.8 0.0 copy-done
  43.8 4.2 %convolution_convert_fusion.1 = bf16[2048,512]{1,0:T(8,128)(2,1)} fusion(bf16[2048,512]{1,0:T(8,128)(2,1)} %get-tuple-element.17, bf16[512,512]{1,0:T(8,128)(2,1)S(1)} %copy-done), kind=kOutput, calls=%fused_computation.1 | convolution fusion | flops 1074790400 | bytes 4718592 | tf_op jit(solution)/shard_map/dot_general | solution.py:427
  48.1 0.0 copy-start.1
  48.1 71.4 %attend.1 = (bf16[8,256,512]{2,1,0:T(8,128)(2,1)}, bf16[512,256]{1,0:T(8,128)(2,1)}, bf16[2,3,512,128]{3,2,1,0:T(8,128)(2,1)}, bf16[4,32,64,128]{3,2,1,0:T(8,128)(2,1)}) custom-call(s32[2]{0:T(128)} %off_ref.5, bf16[512,256]{1,0:T(8,128)(2,1)} %q_ref.1, bf16[2,3,512,128]{3,2,1,0:T(8,128)(2,1)} %get-tuple-element.15.near, ...), custom_call_target="tpu_custom_call" | custom-call | tf_op jit(solution)/shard_map/attend/pallas_call | solution.py:429
  119.5 0.0 copy-done.1
  119.5 0.0 copy-start.2
  119.5 3.8 %convolution_convert_fusion.2 = bf16[512,512]{1,0:T(8,128)(2,1)} fusion(bf16[2048,512]{1,0:T(8,128)(2,1)} %bitcast.10, bf16[2048,512]{1,0:T(8,128)(2,1)S(1)} %copy-done.1), kind=kOutput, calls=%fused_computation.2 | convolution fusion | flops 1074003968 | bytes 4718592 | tf_op jit(solution)/shard_map/dot_general | solution.py:446
  123.3 0.0 copy-done.2
  123.3 2.6 convolution_convert_fusion.wt
  125.9 0.0 copy-start.3
  125.9 148.0 %scatter_grads.1 = (bf16[512,128]{1,0:T(8,128)(2,1)}, bf16[512,128]{1,0:T(8,128)(2,1)}, bf16[256,128]{1,0:T(8,128)(2,1)}) custom-call(s32[2]{0:T(128)} %off_ref.5, bf16[2048,512]{1,0:T(8,128)(2,1)} %convolution_convert_fusion.wt, bf16[4,16,2,64,128]{4,3,2,1,0:T(8,128)(2,1)} %bitcast.9, bf16[2,3,512,128]{3,2,1,0:T(8,128)(2,1)} %get-tuple-element.21.gnear), custom_call_target="tpu_custom_call" | custom-call | tf_op jit(solution)/shard_map/scatter_grads/pallas_call | solution.py:449
  273.9 0.0 copy-done.3
  273.9 0.7 copy.15
  274.6 1.6 copy.16
  276.2 1.6 copy.17
  277.7 1.5 copy.18
Async XLA Ops:
  0.6 43.2 %copy-start = (bf16[512,512]{1,0:T(8,128)(2,1)S(1)}, bf16[512,512]{1,0:T(8,128)(2,1)}, u32[]{:S(2)}) copy-start(bf16[512,512]{1,0:T(8,128)(2,1)} %param.11) | copy-start | bytes 1572868
  48.1 71.4 %copy-start.1 = (bf16[2048,512]{1,0:T(8,128)(2,1)S(1)}, bf16[2048,512]{1,0:T(8,128)(2,1)}, u32[]{:S(2)}) copy-start(bf16[2048,512]{1,0:T(8,128)(2,1)} %get-tuple-element.17) | copy-start | bytes 6291460
  119.5 3.8 %copy-start.2 = (bf16[8,256,512]{2,1,0:T(8,128)(2,1)S(1)}, bf16[8,256,512]{2,1,0:T(8,128)(2,1)}, u32[]{:S(2)}) copy-start(bf16[8,256,512]{2,1,0:T(8,128)(2,1)} %get-tuple-element.18) | copy-start | bytes 6291460
  125.9 148.0 %copy-start.3 = (bf16[512,256]{1,0:T(8,128)(2,1)S(1)}, bf16[512,256]{1,0:T(8,128)(2,1)}, u32[]{:S(2)}) copy-start(bf16[512,256]{1,0:T(8,128)(2,1)} %get-tuple-element.31) | copy-start | bytes 786436

commit v2 on v1

v2 whole, which is shorter than its diff:
```python
import jax
import jax.numpy as jnp
from jax import lax
from jax.experimental import pallas as pl
from jax.experimental.pallas import tpu as pltpu
from jax.sharding import PartitionSpec as P

T = 512
DH = 128
BLK = 64
NH = 8
NC = 32
SCALE = DH ** -0.5
EXP2_SCALE = SCALE * 1.4426950408889634
NEG = -1e30
MESH = pl.DeviceIdType.MESH
BF = jnp.bfloat16
F32 = jnp.float32


def where_am_i():
    c = lax.axis_index("ctx")
    h = lax.axis_index("head")
    return c, h, c // 4, (c // 2) % 2, c % 2


def ctx_id(z, yh, core):
    return z * 4 + yh * 2 + core


def across(h):
    return h + 1 - 2 * lax.rem(h, 2)


def head_peers(h):
    return lax.rem(h + 2, NH), lax.rem(h + NH - 2, NH), across(h)


def signal(barrier, c, h):
    pl.semaphore_signal(barrier, inc=1, device_id=(c, h), device_id_type=MESH)


class Sends:
    def __init__(self, sems):
        self.sems, self.made = sems, []

    def start(self, src, dst, recv, c, h):
        copy = pltpu.make_async_remote_copy(
            src_ref=src, dst_ref=dst, send_sem=self.sems.at[len(self.made)],
            recv_sem=recv, device_id=(c, h), device_id_type=MESH)
        copy.start()
        self.made.append(copy)

    def finish(self):
        for copy in self.made:
            copy.wait_send()


def arrived(ref, recv, send, c, h):
    pltpu.make_async_remote_copy(
        src_ref=ref, dst_ref=ref, send_sem=send, recv_sem=recv,
        device_id=(c, h), device_id_type=MESH).wait_recv()


def fold(x, op):
    return op(x.reshape(T // 8, 8, T), axis=0)


def nt(a, b):
    return lax.dot_general(a, b, (((1,), (1,)), ((), ())), preferred_element_type=F32)


def tn(a, b):
    return lax.dot_general(a, b, (((0,), (0,)), ((), ())), preferred_element_type=F32)


def nn(a, b):
    return jnp.dot(a, b, preferred_element_type=F32)


def step_kernel(off_ref, q_ref, k_ref, v_ref, g_ref, w_ref,
                lo_ref, gq_ref, gk_ref, gv_ref, gw_ref,
                picked, near, fg, att_all, wc, gpick, gnear,
                qs, scores, probs, dnear, top, inv, acc, dog, gatt,
                wts, pair_w, wup, wdown, wdone, wslot,
                pair_p, mine, up, down, done, yslot, brecv, csum, crecv,
                send, pk_recv, g_recv, c_recv, b_recv, w_recv, a_recv,
                pw_recv, wup_recv, wdown_recv, pp_recv, up_recv, down_recv,
                y_recv, near_recv, local):
    c, h, z, yh, core = where_am_i()
    partner = c + 1 - 2 * core
    ypeer = ctx_id(z, 1 - yh, core)
    after, before = lax.rem(c + 2, NC), lax.rem(c + NC - 2, NC)
    above = ctx_id(lax.rem(z + 1, 8), yh, core)
    below = ctx_id(lax.rem(z + 7, 8), yh, core)
    east, west, side = head_peers(h)
    west_side, east_side, far = across(west), across(east), head_peers(east)[0]
    far_side = across(far)
    hs = [lax.rem(h + d, NH) for d in range(1, NH)]
    barrier = pltpu.get_barrier_semaphore()

    def owner(d, y):
        return ctx_id(lax.rem(z + d, 8), lax.rem(yh + y, 2), core)

    for peer in (partner, ypeer, after, before, above, below):
        signal(barrier, peer, h)
    for peer in hs:
        signal(barrier, c, peer)
    for r in range(2):
        wanted = jnp.full((BLK, DH), 7 - off_ref[r], jnp.int32)
        for source, slot in ((k_ref, r), (v_ref, 2 + r)):
            rows = source[:BLK].astype(F32)
            for b in range(1, 8):
                rows = jnp.where(wanted == b, source[b * BLK:(b + 1) * BLK].astype(F32), rows)
            picked[slot, c] = rows.astype(BF)
    copies = [
        pltpu.make_async_copy(k_ref, near.at[0, 0], local.at[0]),
        pltpu.make_async_copy(v_ref, near.at[1, 0], local.at[1]),
        pltpu.make_async_copy(g_ref, fg.at[h], local.at[2]),
        pltpu.make_async_copy(
            w_ref.at[:, pl.ds(pl.multiple_of(h * T, T), T)],
            wc.at[pl.ds(pl.multiple_of(h * 256, 256), 256), :], local.at[3]),
    ]
    for copy in copies:
        copy.start()
    for r in range(2):
        qs[r] = q_ref[:, r * DH:(r + 1) * DH]
    dnear[...] = jnp.zeros_like(dnear)
    pl.semaphore_wait(barrier, 13)

    sends = Sends(send)

    def block(t):
        return picked.at[:, t]

    def pass_on(t, *peers):
        for peer in peers:
            sends.start(block(t), block(t), pk_recv.at[t], peer, h)

    def take(t, peer):
        arrived(block(t), pk_recv.at[t], send.at[0], peer, h)

    def gpart(n, half):
        return fg.at[n, pl.ds(half * 256, 256)]

    def own_part(half, peer):
        sends.start(g_ref.at[pl.ds(half * 256, 256)], gpart(h, half), g_recv.at[h, half], c, peer)

    def grelay(n, half, source, *peers):
        arrived(gpart(n, half), g_recv.at[n, half], send.at[0], c, source)
        for peer in peers:
            sends.start(gpart(n, half), gpart(n, half), g_recv.at[n, half], c, peer)

    def pick_ring(step):
        for y in range(2):
            t = owner(8 - step, y)
            take(t, below)
            pass_on(t, *((above, partner) if step < 4 else (partner,)))
            if step < 4:
                t = owner(step, y)
                take(t, above)
                pass_on(t, *((below, partner) if step < 3 else (partner,)))

    pass_on(c, ypeer, above, below, partner)
    own_part(0, east)
    own_part(1, west)
    own_part(0, side)
    sends.start(k_ref, near.at[0, 2], c_recv.at[0], after, h)
    sends.start(v_ref, near.at[1, 2], c_recv.at[1], after, h)
    own_part(1, east)
    own_part(0, west)
    own_part(1, side)
    take(ypeer, ypeer)
    pass_on(ypeer, above, below, partner)
    pick_ring(1)
    grelay(side, 0, side, east, west)
    grelay(west, 0, west, east)
    grelay(east, 1, east, west)
    pick_ring(2)
    pick_ring(3)
    grelay(side, 1, side, west, east)
    pick_ring(4)
    for n in range(2):
        arrived(near.at[n, 2], c_recv.at[n], send.at[0], before, h)
    for copy in copies:
        copy.wait()
    for n in range(2):
        sends.start(near.at[n, 2 * core], near.at[n, 1], b_recv.at[n], partner, h)
    grelay(west_side, 0, west, east)
    grelay(east_side, 1, east, west)
    flip = 1 - 2 * core
    for d in range(8):
        for y in range(2):
            t = owner(d, y) + flip
            take(t, partner)
    for n in range(2):
        arrived(near.at[n, 1], b_recv.at[n], send.at[0], partner, h)

    def tile(p):
        return pl.ds(pl.multiple_of(p * 8, 8), 8)

    def forward(r):
        q = qs[r]
        key = lax.broadcasted_iota(jnp.int32, (T, T), 0)
        query = lax.broadcasted_iota(jnp.int32, (T, T), 1)
        s = jnp.where(key <= query, nt(near[0, 0], q), NEG)
        scores[0] = s
        top[...] = fold(s, jnp.max)
        s = jnp.where(c >= 1, nt(near[0, 1], q), NEG)
        scores[1] = s
        top[...] = jnp.maximum(top[...], fold(s, jnp.max))
        kb, qb = key // BLK, query // BLK
        ok = ((kb > qb) | (kb == 7 - off_ref[r])) & (c >= 2)
        s = jnp.where(ok, nt(near[0, 2], q), NEG)
        scores[2] = s
        top[...] = jnp.maximum(top[...], fold(s, jnp.max))

        def pick_scores(p, _):
            rows = lax.broadcasted_iota(jnp.int32, (T, T), 0)
            s = nt(picked[r, tile(p)].reshape(T, DH), q)
            s = jnp.where(rows < (c - 2) * BLK - p * T, s, NEG)
            scores[3 + p] = s
            top[...] = jnp.maximum(top[...], fold(s, jnp.max))
            return 0

        lax.fori_loop(0, 4, pick_scores, 0)
        m = jnp.max(top[...], axis=0, keepdims=True)
        top[...] = jnp.zeros_like(top)
        acc[...] = jnp.zeros_like(acc)

        def weigh(i, values):
            w = jnp.exp2((scores[i] - m) * EXP2_SCALE)
            top[...] += fold(w, jnp.sum)
            w = w.astype(BF)
            probs[r, i] = w
            acc[...] += tn(values, w)

        def near_mix(i, _):
            weigh(i, near[1, i])
            return 0

        def pick_mix(p, _):
            weigh(3 + p, picked[2 + r, tile(p)].reshape(T, DH))
            return 0

        lax.fori_loop(0, 3, near_mix, 0)
        lax.fori_loop(0, 4, pick_mix, 0)
        total = 1.0 / jnp.sum(top[...], axis=0, keepdims=True)
        inv[r] = jnp.broadcast_to(total, (8, T))
        att_all[h, pl.ds(r * DH, DH), :] = (acc[...] * total).astype(BF)

    def part(n, half):
        return att_all.at[n, pl.ds(half * DH, DH)]

    def relay(n, half, source, *peers):
        if source is not None:
            arrived(part(n, half), a_recv.at[n, half], send.at[0], c, source)
        for peer in peers:
            sends.start(part(n, half), part(n, half), a_recv.at[n, half], c, peer)

    def piece(half, r):
        return wc.at[pl.ds(pl.multiple_of(r * 256, 256), 256),
                     pl.ds(pl.multiple_of(half * 256, 256), 256)]

    forward(0)
    relay(h, 0, None, east, side, west)
    forward(1)
    relay(h, 1, None, west, side, east)
    for n, half, source in (
            (west, 1, west), (east, 0, east), (west_side, 1, west), (east_side, 0, east),
            (far, 0, west), (far, 1, east), (far_side, 0, west), (far_side, 1, east)):
        grelay(n, half, source)

    order = [lax.rem(z + d, 8) for d in (4, 5, 3, 6, 2, 7, 1, 0)]
    for t in order:
        term = nn(att_all[h], fg[t])
        for j in range(4):
            wts[t, j % 2, j // 2] = term[:, j * DH:(j + 1) * DH].astype(BF)
        sends.start(wts.at[t, 1 - core], pair_w.at[t], pw_recv.at[t], partner, h)

    def quad(p):
        return pl.ds(pl.multiple_of(p * 4, 4), 4)

    def combine(t):
        arrived(pair_w.at[t], pw_recv.at[t], send.at[0], partner, h)
        wts[t, core] = (wts[t, core].astype(F32) + pair_w[t].astype(F32)).astype(BF)

    def grads(r, i, keys, values, rowdot):
        w = probs[r, i]
        do = dog[...]
        dp = nt(values, do)
        ds = (w.astype(F32) * (dp - rowdot)).astype(BF)
        acc[...] += tn(keys, ds)
        return nn(ds, qs[r]) * SCALE, nn(w, do)

    def start_backward(r):
        rows = pl.ds(r * DH, DH)
        grad = gatt[rows, :].astype(BF).astype(F32)
        total = inv[r, 0:1]
        dog[...] = (grad * total).T.astype(BF)
        acc[...] = jnp.zeros_like(acc)
        return jnp.sum(grad * att_all[h, rows, :].astype(F32), axis=0, keepdims=True) * total

    def backward_near(r, rowdot):
        def near_grads(i, _):
            dk, dv = grads(r, i, near[0, i], near[1, i], rowdot)
            dnear[0, i] += dk
            dnear[1, i] += dv
            return 0

        lax.fori_loop(0, 3, near_grads, 0)

    def backward_pick(r, rowdot):
        def pick_grads(p, _):
            dk, dv = grads(r, 3 + p, picked[r, tile(p)].reshape(T, DH),
                           picked[2 + r, tile(p)].reshape(T, DH), rowdot)
            gpick[r, 0, quad(p)] = dk.astype(BF).reshape(4, 2, BLK, DH)
            gpick[r, 1, quad(p)] = dv.astype(BF).reshape(4, 2, BLK, DH)
            return 0

        lax.fori_loop(0, 4, pick_grads, 0)
        gq_ref[:, r * DH:(r + 1) * DH] = (acc[...].T * SCALE).astype(BF)

    def w_ring(step):
        t = order[2 + 2 * step]
        combine(t)
        arrived(wup.at[step], wup_recv.at[step], send.at[0], below, h)
        wup[step] = (wup[step].astype(F32) + wts[t, core].astype(F32)).astype(BF)
        sends.start(wup.at[step], wup.at[step + 1], wup_recv.at[step + 1], above, h)
        t = order[3 + 2 * step]
        combine(t)
        if step < 2:
            arrived(wdown.at[step], wdown_recv.at[step], send.at[0], above, h)
            wdown[step] = (wdown[step].astype(F32) + wts[t, core].astype(F32)).astype(BF)
            sends.start(wdown.at[step], wdown.at[step + 1], wdown_recv.at[step + 1], below, h)

    def pair(t):
        return pl.ds(pl.multiple_of(t * 2, 2), 2)

    def share_picks(r):
        for t in order:
            sends.start(gpick.at[r, :, pair(t), 1 - core], pair_p.at[r, t], pp_recv.at[r, t],
                        partner, h)

    def combine_picks(r, t):
        arrived(pair_p.at[r, t], pp_recv.at[r, t], send.at[0], partner, h)
        for y in range(2):
            own = gpick[r, :, t * 2 + y, core].astype(F32) + pair_p[r, t, :, y].astype(F32)
            mine[r, t, y] = own.astype(BF).reshape(DH, DH)

    def open_ring(r):
        combine_picks(r, order[0])
        sends.start(mine.at[r, order[0]], up.at[r, 0], up_recv.at[r, 0], above, h)
        combine_picks(r, order[1])
        sends.start(mine.at[r, order[1]], down.at[r, 0], down_recv.at[r, 0], below, h)

    def sum_ring(r, step):
        t = order[2 + 2 * step]
        combine_picks(r, t)
        arrived(up.at[r, step], up_recv.at[r, step], send.at[0], below, h)
        up[r, step] = (up[r, step].astype(F32) + mine[r, t].astype(F32)).astype(BF)
        sends.start(up.at[r, step], up.at[r, step + 1], up_recv.at[r, step + 1], above, h)
        t = order[3 + 2 * step]
        combine_picks(r, t)
        if step < 2:
            arrived(down.at[r, step], down_recv.at[r, step], send.at[0], above, h)
            down[r, step] = (down[r, step].astype(F32) + mine[r, t].astype(F32)).astype(BF)
            sends.start(down.at[r, step], down.at[r, step + 1], down_recv.at[r, step + 1],
                        below, h)

    def close_ring(r):
        arrived(down.at[r, 2], down_recv.at[r, 2], send.at[0], above, h)
        arrived(up.at[r, 3], up_recv.at[r, 3], send.at[0], below, h)
        done[r] = (mine[r, z].astype(F32) + up[r, 3].astype(F32)
                   + down[r, 2].astype(F32)).astype(BF)
        sends.start(done.at[r, 1 - yh], yslot.at[r], y_recv.at[r], ypeer, h)

    gatt[...] = jnp.zeros_like(gatt)

    def grad_att(r, _):
        gatt[...] += nt(w_ref[:, pl.ds(pl.multiple_of(r * T, T), T)], fg[r])
        return 0

    lax.fori_loop(0, NH, grad_att, 0)
    rowdot = start_backward(0)
    relay(side, 0, side, east, west)
    relay(west, 0, west, east)
    combine(order[0])
    sends.start(wts.at[order[0], core], wup.at[0], wup_recv.at[0], above, h)
    combine(order[1])
    sends.start(wts.at[order[1], core], wdown.at[0], wdown_recv.at[0], below, h)
    backward_near(0, rowdot)
    relay(side, 1, side, west, east)
    relay(east, 1, east, west)
    w_ring(0)
    for peer in hs:
        sends.start(w_ref.at[:, pl.ds(pl.multiple_of(peer * T + core * 256, 256), 256)],
                    piece(core, h), w_recv.at[core, h], c, peer)
    backward_pick(0, rowdot)
    share_picks(0)
    relay(west_side, 0, west, east)
    relay(east_side, 1, east, west)
    w_ring(1)
    rowdot = start_backward(1)
    backward_near(1, rowdot)
    gnear[...] = dnear[...].astype(BF)
    sends.start(gnear.at[:, 1], brecv, near_recv.at[0], partner, h)
    w_ring(2)
    open_ring(0)
    backward_pick(1, rowdot)
    share_picks(1)
    sum_ring(0, 0)
    arrived(wdown.at[2], wdown_recv.at[2], send.at[0], above, h)
    arrived(wup.at[3], wup_recv.at[3], send.at[0], below, h)
    wdone[...] = (wts[z, core].astype(F32) + wup[3].astype(F32)
                  + wdown[2].astype(F32)).astype(BF)
    sends.start(wdone.at[1 - yh], wslot, y_recv.at[2], ypeer, h)
    open_ring(1)
    arrived(brecv, near_recv.at[0], send.at[0], partner, h)
    extra = brecv[...].astype(F32)
    csum[...] = (gnear[:, 2].astype(F32) + jnp.where(core == 1, extra, 0.0)).astype(BF)
    sends.start(csum, crecv, near_recv.at[1], before, h)
    sum_ring(0, 1)
    for peer in hs:
        arrived(piece(core, peer), w_recv.at[core, peer], send.at[0], c, peer)
        sends.start(piece(core, peer), piece(core, peer), w_recv.at[core, peer], partner, h)
    sum_ring(1, 0)
    sum_ring(0, 2)
    relay(west, 1, west)
    relay(east, 0, east)
    relay(west_side, 1, west)
    relay(east_side, 0, east)
    relay(far, 0, west)
    relay(far, 1, east)
    relay(far_side, 0, west)
    relay(far_side, 1, east)
    sum_ring(1, 1)
    close_ring(0)
    for peer in hs:
        arrived(piece(1 - core, peer), w_recv.at[1 - core, peer], send.at[0], partner, h)
    scores[0] = jnp.zeros((T, T), F32)

    def project(r, _):
        scores[0] += tn(att_all[r], wc[pl.ds(pl.multiple_of(r * 256, 256), 256), :])
        return 0

    lax.fori_loop(0, 4, project, 0)
    sum_ring(1, 2)
    lax.fori_loop(4, NH, project, 0)
    close_ring(1)
    lo_ref[...] = scores[0].astype(BF)
    arrived(wslot, y_recv.at[2], send.at[0], ypeer, h)
    gw_ref[...] = (wdone[yh].astype(F32) + wslot[...].astype(F32)).astype(BF)
    arrived(crecv, near_recv.at[1], send.at[0], after, h)
    grad = gnear[:, 0].astype(F32) + jnp.where(core == 1, 0.0, extra) + crecv[...].astype(F32)
    block = lax.broadcasted_iota(jnp.int32, (T, DH), 0) // BLK
    grads_out = [grad[0], grad[1]]
    for r in range(2):
        arrived(yslot.at[r], y_recv.at[r], send.at[0], ypeer, h)
        total = done[r, yh].astype(F32) + yslot[r].astype(F32)
        for n in range(2):
            spread = jnp.concatenate([total[n * BLK:(n + 1) * BLK]] * 8, axis=0)
            grads_out[n] += jnp.where(block == 7 - off_ref[r], spread, 0.0)
    gk_ref[...] = grads_out[0].astype(BF)
    gv_ref[...] = grads_out[1].astype(BF)
    sends.finish()


def hand_over(*refs):
    for source, target in zip(refs[:5], refs[5:]):
        target[...] = source[...]


VM = pl.BlockSpec(memory_space=pltpu.VMEM)
SM = pl.BlockSpec(memory_space=pltpu.SMEM)
DMA = pltpu.SemaphoreType.DMA


def shaped(*shape, dtype=BF):
    return jax.ShapeDtypeStruct(shape, dtype)


def params(number):
    return pltpu.CompilerParams(
        collective_id=number, has_side_effects=True, vmem_limit_bytes=60 << 20)


def buf(*shape, dtype=BF):
    return pltpu.VMEM(shape, dtype)


def body(queries, keys, values, stride_offset, w_out, grad_out):
    shapes = (shaped(T, T), shaped(T, 256), shaped(T, DH), shaped(T, DH), shaped(256, DH))
    results = pl.pallas_call(
        step_kernel,
        out_shape=shapes,
        in_specs=[SM, VM, VM, VM, VM, VM],
        out_specs=(VM,) * 5,
        scratch_shapes=[
            buf(4, NC, BLK, DH), buf(2, 3, T, DH), buf(NH, T, T), buf(NH, 256, T),
            buf(2048, T), buf(2, 2, 16, 2, BLK, DH), buf(2, 3, T, DH),
            buf(2, T, DH), buf(7, T, T, dtype=F32), buf(2, 7, T, T),
            buf(2, 3, T, DH, dtype=F32), buf(8, T, dtype=F32), buf(2, 8, T, dtype=F32),
            buf(DH, T, dtype=F32), buf(T, DH), buf(256, T, dtype=F32),
            buf(8, 2, 2, 256, DH), buf(8, 2, 256, DH), buf(4, 2, 256, DH), buf(3, 2, 256, DH),
            buf(2, 256, DH), buf(256, DH),
            buf(2, 8, 2, 2, BLK, DH), buf(2, 8, 2, DH, DH), buf(2, 4, 2, DH, DH),
            buf(2, 3, 2, DH, DH), buf(2, 2, DH, DH), buf(2, DH, DH),
            buf(2, T, DH), buf(2, T, DH), buf(2, T, DH),
            DMA((140,)), DMA((NC,)), DMA((NH, 2)), DMA((2,)), DMA((2,)), DMA((2, NH)),
            DMA((NH, 2)), DMA((8,)), DMA((4,)), DMA((3,)), DMA((2, 8)), DMA((2, 4)),
            DMA((2, 3)), DMA((3,)), DMA((2,)), DMA((4,)),
        ],
        compiler_params=params(0),
        name="step",
    )(stride_offset, queries, keys, values, grad_out, w_out)
    return pl.pallas_call(
        hand_over, out_shape=shapes, in_specs=[VM] * 5, out_specs=(VM,) * 5, name="hand_over",
    )(*results)


def solution(mesh):
    return jax.shard_map(
        body,
        mesh=mesh,
        in_specs=(P("ctx", "head"), P("ctx", "head"), P("ctx", "head"), P("head"),
                  P("head", None), P("ctx", "head")),
        out_specs=(P("ctx", "head"), P("ctx", "head"), P("ctx", "head"), P("ctx", "head"),
                   P("head", "ctx")),
        check_vma=False,
    )
```

time: 284 us -> 105 us (0.37); the launches traced: 279 us -> 105 us
  Pallas kernels: 263 us -> 104 us
  matrix products: 10.6 us -> 0 us
  local copies, waits for them, and re-layouts: 5.33 us -> 0 us
    pallas_call x3 -> x2, Pallas kernels: 263 us -> 104 us  [the longest x1 102 us: body(): pl.pallas_call(step_kernel, out_shape=shapes, in_specs=[SM, VM, VM, VM, V...]
    dot_general x3 -> x0, matrix products: 10.6 us -> none  [the longest x1 4.24 us: body(): lax.dot_general(wc, grad_out, (((1,), (1,)), ((), ())), preferred_element...]
    unnamed x12 -> x0, local copies, waits for them, and re-layouts: 5.33 us -> none
where the time goes in v2:
time: 105 us
  Pallas kernels  104 us (99%)
    pallas_call x1, Pallas kernels, body(): pl.pallas_call(step_kernel, out_shape=shapes, in_specs=[SM, VM, VM, VM, V...  102 us
    pallas_call x1, Pallas kernels, body(): pl.pallas_call(hand_over, out_shape=shapes, in_specs=[VM] * 5, out_specs=...  2.2 us

profile of v2, /device:TPU:14, one launch (start us, length us, event | category | flops | bytes accessed | tf_op | source)
XLA Modules:
  0.0 105.0 jit_solution(11488997202266973078)
XLA Ops:
  0.6 102.1 %step.1 = (bf16[512,512]{1,0:T(8,128)(2,1)}, bf16[512,256]{1,0:T(8,128)(2,1)}, bf16[512,128]{1,0:T(8,128)(2,1)}, bf16[512,128]{1,0:T(8,128)(2,1)}, bf16[256,128]{1,0:T(8,128)(2,1)}) custom-call(s32[2]{0:T(128)} %off_ref.1, bf16[512,256]{1,0:T(8,128)(2,1)} %q_ref.1, bf16[512,128]{1,0:T(8,128)(2,1)} %k_ref.1, bf16[512,128]{1,0:T(8,128)(2,1)} %v_ref.1, ...), custom_call_target="tpu_custom_call" | custom-call | tf_op jit(solution)/shard_map/step/pallas_call | solution.py:494
  102.8 2.2 %hand_over.1 = (bf16[512,512]{1,0:T(8,128)(2,1)}, bf16[512,256]{1,0:T(8,128)(2,1)}, bf16[512,128]{1,0:T(8,128)(2,1)}, bf16[512,128]{1,0:T(8,128)(2,1)}, bf16[256,128]{1,0:T(8,128)(2,1)}) custom-call(bf16[512,512]{1,0:T(8,128)(2,1)} %get-tuple-element.10.refs_0_, bf16[512,256]{1,0:T(8,128)(2,1)} %get-tuple-element.11.refs_1_, ...), custom_call_target="tpu_custom_call" | custom-call | tf_op jit(solution)/shard_map/hand_over/pallas_call | solution.py:517

commit v3 on v2

--- a/solution.py
+++ b/solution.py
@@ -81,7 +81,7 @@
 def step_kernel(off_ref, q_ref, k_ref, v_ref, g_ref, w_ref,
                 lo_ref, gq_ref, gk_ref, gv_ref, gw_ref,
                 picked, near, fg, att_all, wc, gpick, gnear,
-                qs, scores, probs, dnear, top, inv, acc, dog, gatt,
+                qs, scores, probs, dnear, top, inv, acc, dog, gatt, rdot,
                 wts, pair_w, wup, wdown, wdone, wslot,
                 pair_p, mine, up, down, done, yslot, brecv, csum, crecv,
                 send, pk_recv, g_recv, c_recv, b_recv, w_recv, a_recv,
@@ -126,6 +126,71 @@
     for r in range(2):
         qs[r] = q_ref[:, r * DH:(r + 1) * DH]
     dnear[...] = jnp.zeros_like(dnear)
+    def tile(p):
+        return pl.ds(pl.multiple_of(p * 8, 8), 8)
+
+    def own_scores(r):
+        key = lax.broadcasted_iota(jnp.int32, (T, T), 0)
+        query = lax.broadcasted_iota(jnp.int32, (T, T), 1)
+        s = jnp.where(key <= query, nt(k_ref[...], qs[r]), NEG)
+        scores[r, 0] = s
+        top[r] = fold(s, jnp.max)
+
+    def last_scores(r):
+        s = jnp.where(c >= 1, nt(near[0, 1], qs[r]), NEG)
+        scores[r, 1] = s
+        top[r] = jnp.maximum(top[r], fold(s, jnp.max))
+
+    def edge_scores(r):
+        kb = lax.broadcasted_iota(jnp.int32, (T, T), 0) // BLK
+        qb = lax.broadcasted_iota(jnp.int32, (T, T), 1) // BLK
+        ok = ((kb > qb) | (kb == 7 - off_ref[r])) & (c >= 2)
+        s = jnp.where(ok, nt(near[0, 2], qs[r]), NEG)
+        scores[r, 2] = s
+        top[r] = jnp.maximum(top[r], fold(s, jnp.max))
+
+    def forward(r):
+        def pick_scores(p, _):
+            rows = lax.broadcasted_iota(jnp.int32, (T, T), 0)
+            s = nt(picked[r, tile(p)].reshape(T, DH), qs[r])
+            s = jnp.where(rows < (c - 2) * BLK - p * T, s, NEG)
+            scores[r, 3 + p] = s
+            top[r] = jnp.maximum(top[r], fold(s, jnp.max))
+            return 0
+
+        lax.fori_loop(0, 4, pick_scores, 0)
+        m = jnp.max(top[r], axis=0, keepdims=True)
+        top[r] = jnp.zeros((8, T), F32)
+        acc[r] = jnp.zeros((DH, T), F32)
+
+        def weigh(i, values):
+            w = jnp.exp2((scores[r, i] - m) * EXP2_SCALE)
+            top[r] += fold(w, jnp.sum)
+            w = w.astype(BF)
+            probs[r, i] = w
+            acc[r] += tn(values, w)
+
+        def near_mix(i, _):
+            weigh(i, near[1, i])
+            return 0
+
+        def pick_mix(p, _):
+            weigh(3 + p, picked[2 + r, tile(p)].reshape(T, DH))
+            return 0
+
+        lax.fori_loop(0, 3, near_mix, 0)
+        lax.fori_loop(0, 4, pick_mix, 0)
+        total = 1.0 / jnp.sum(top[r], axis=0, keepdims=True)
+        inv[r] = jnp.broadcast_to(total, (8, T))
+        att_all[h, pl.ds(r * DH, DH), :] = (acc[r] * total).astype(BF)
+
+    def grad_att(r, block):
+        gatt[...] += nt(w_ref[:, pl.ds(pl.multiple_of(r * T, T), T)], block)
+
+    own_scores(0)
+    own_scores(1)
+    gatt[...] = jnp.zeros_like(gatt)
+    grad_att(h, g_ref[...])
     pl.semaphore_wait(barrier, 13)
 
     sends = Sends(send)
@@ -177,77 +242,29 @@
     grelay(west, 0, west, east)
     grelay(east, 1, east, west)
     pick_ring(2)
-    pick_ring(3)
-    grelay(side, 1, side, west, east)
-    pick_ring(4)
     for n in range(2):
         arrived(near.at[n, 2], c_recv.at[n], send.at[0], before, h)
     for copy in copies:
         copy.wait()
     for n in range(2):
         sends.start(near.at[n, 2 * core], near.at[n, 1], b_recv.at[n], partner, h)
+    edge_scores(0)
+    pick_ring(3)
+    edge_scores(1)
+    grelay(side, 1, side, west, east)
+    grad_att(side, fg[side])
+    pick_ring(4)
     grelay(west_side, 0, west, east)
     grelay(east_side, 1, east, west)
     flip = 1 - 2 * core
+    for n in range(2):
+        arrived(near.at[n, 1], b_recv.at[n], send.at[0], partner, h)
+    last_scores(0)
+    last_scores(1)
     for d in range(8):
         for y in range(2):
             t = owner(d, y) + flip
             take(t, partner)
-    for n in range(2):
-        arrived(near.at[n, 1], b_recv.at[n], send.at[0], partner, h)
-
-    def tile(p):
-        return pl.ds(pl.multiple_of(p * 8, 8), 8)
-
-    def forward(r):
-        q = qs[r]
-        key = lax.broadcasted_iota(jnp.int32, (T, T), 0)
-        query = lax.broadcasted_iota(jnp.int32, (T, T), 1)
-        s = jnp.where(key <= query, nt(near[0, 0], q), NEG)
-        scores[0] = s
-        top[...] = fold(s, jnp.max)
-        s = jnp.where(c >= 1, nt(near[0, 1], q), NEG)
-        scores[1] = s
-        top[...] = jnp.maximum(top[...], fold(s, jnp.max))
-        kb, qb = key // BLK, query // BLK
-        ok = ((kb > qb) | (kb == 7 - off_ref[r])) & (c >= 2)
-        s = jnp.where(ok, nt(near[0, 2], q), NEG)
-        scores[2] = s
-        top[...] = jnp.maximum(top[...], fold(s, jnp.max))
-
-        def pick_scores(p, _):
-            rows = lax.broadcasted_iota(jnp.int32, (T, T), 0)
-            s = nt(picked[r, tile(p)].reshape(T, DH), q)
-            s = jnp.where(rows < (c - 2) * BLK - p * T, s, NEG)
-            scores[3 + p] = s
-            top[...] = jnp.maximum(top[...], fold(s, jnp.max))
-            return 0
-
-        lax.fori_loop(0, 4, pick_scores, 0)
-        m = jnp.max(top[...], axis=0, keepdims=True)
-        top[...] = jnp.zeros_like(top)
-        acc[...] = jnp.zeros_like(acc)
-
-        def weigh(i, values):
-            w = jnp.exp2((scores[i] - m) * EXP2_SCALE)
-            top[...] += fold(w, jnp.sum)
-            w = w.astype(BF)
-            probs[r, i] = w
-            acc[...] += tn(values, w)
-
-        def near_mix(i, _):
-            weigh(i, near[1, i])
-            return 0
-
-        def pick_mix(p, _):
-            weigh(3 + p, picked[2 + r, tile(p)].reshape(T, DH))
-            return 0
-
-        lax.fori_loop(0, 3, near_mix, 0)
-        lax.fori_loop(0, 4, pick_mix, 0)
-        total = 1.0 / jnp.sum(top[...], axis=0, keepdims=True)
-        inv[r] = jnp.broadcast_to(total, (8, T))
-        att_all[h, pl.ds(r * DH, DH), :] = (acc[...] * total).astype(BF)
 
     def part(n, half):
         return att_all.at[n, pl.ds(half * DH, DH)]
@@ -270,6 +287,8 @@
             (west, 1, west), (east, 0, east), (west_side, 1, west), (east_side, 0, east),
             (far, 0, west), (far, 1, east), (far_side, 0, west), (far_side, 1, east)):
         grelay(n, half, source)
+    for n in (west, east, west_side, east_side, far, far_side):
+        grad_att(n, fg[n])
 
     order = [lax.rem(z + d, 8) for d in (4, 5, 3, 6, 2, 7, 1, 0)]
     for t in order:
@@ -285,41 +304,41 @@
         arrived(pair_w.at[t], pw_recv.at[t], send.at[0], partner, h)
         wts[t, core] = (wts[t, core].astype(F32) + pair_w[t].astype(F32)).astype(BF)
 
-    def grads(r, i, keys, values, rowdot):
+    def grads(r, i, keys, values):
         w = probs[r, i]
-        do = dog[...]
+        do = dog[r]
         dp = nt(values, do)
-        ds = (w.astype(F32) * (dp - rowdot)).astype(BF)
-        acc[...] += tn(keys, ds)
+        ds = (w.astype(F32) * (dp - rdot[r, 0:1])).astype(BF)
+        acc[r] += tn(keys, ds)
         return nn(ds, qs[r]) * SCALE, nn(w, do)
 
     def start_backward(r):
         rows = pl.ds(r * DH, DH)
         grad = gatt[rows, :].astype(BF).astype(F32)
         total = inv[r, 0:1]
-        dog[...] = (grad * total).T.astype(BF)
-        acc[...] = jnp.zeros_like(acc)
-        return jnp.sum(grad * att_all[h, rows, :].astype(F32), axis=0, keepdims=True) * total
-
-    def backward_near(r, rowdot):
+        dog[r] = (grad * total).T.astype(BF)
+        acc[r] = jnp.zeros((DH, T), F32)
+        rdot[r] = jnp.broadcast_to(
+            jnp.sum(grad * att_all[h, rows, :].astype(F32), axis=0, keepdims=True) * total, (8, T))
+
+    def backward_near(r, first, last):
         def near_grads(i, _):
-            dk, dv = grads(r, i, near[0, i], near[1, i], rowdot)
+            dk, dv = grads(r, i, near[0, i], near[1, i])
             dnear[0, i] += dk
             dnear[1, i] += dv
             return 0
 
-        lax.fori_loop(0, 3, near_grads, 0)
-
-    def backward_pick(r, rowdot):
+        lax.fori_loop(first, last, near_grads, 0)
+
+    def backward_pick(r):
         def pick_grads(p, _):
             dk, dv = grads(r, 3 + p, picked[r, tile(p)].reshape(T, DH),
-                           picked[2 + r, tile(p)].reshape(T, DH), rowdot)
+                           picked[2 + r, tile(p)].reshape(T, DH))
             gpick[r, 0, quad(p)] = dk.astype(BF).reshape(4, 2, BLK, DH)
             gpick[r, 1, quad(p)] = dv.astype(BF).reshape(4, 2, BLK, DH)
             return 0
 
         lax.fori_loop(0, 4, pick_grads, 0)
-        gq_ref[:, r * DH:(r + 1) * DH] = (acc[...].T * SCALE).astype(BF)
 
     def w_ring(step):
         t = order[2 + 2 * step]
@@ -375,56 +394,53 @@
                    + down[r, 2].astype(F32)).astype(BF)
         sends.start(done.at[r, 1 - yh], yslot.at[r], y_recv.at[r], ypeer, h)
 
-    gatt[...] = jnp.zeros_like(gatt)
-
-    def grad_att(r, _):
-        gatt[...] += nt(w_ref[:, pl.ds(pl.multiple_of(r * T, T), T)], fg[r])
-        return 0
-
-    lax.fori_loop(0, NH, grad_att, 0)
-    rowdot = start_backward(0)
+    start_backward(0)
     relay(side, 0, side, east, west)
     relay(west, 0, west, east)
     combine(order[0])
     sends.start(wts.at[order[0], core], wup.at[0], wup_recv.at[0], above, h)
     combine(order[1])
     sends.start(wts.at[order[1], core], wdown.at[0], wdown_recv.at[0], below, h)
-    backward_near(0, rowdot)
+    backward_pick(0)
+    share_picks(0)
     relay(side, 1, side, west, east)
     relay(east, 1, east, west)
     w_ring(0)
     for peer in hs:
         sends.start(w_ref.at[:, pl.ds(pl.multiple_of(peer * T + core * 256, 256), 256)],
                     piece(core, h), w_recv.at[core, h], c, peer)
-    backward_pick(0, rowdot)
-    share_picks(0)
+    backward_near(0, 1, 3)
     relay(west_side, 0, west, east)
     relay(east_side, 1, east, west)
     w_ring(1)
-    rowdot = start_backward(1)
-    backward_near(1, rowdot)
-    gnear[...] = dnear[...].astype(BF)
+    open_ring(0)
+    start_backward(1)
+    backward_pick(1)
+    share_picks(1)
+    w_ring(2)
+    sum_ring(0, 0)
+    backward_near(1, 1, 3)
+    gnear[:, 1:] = dnear[:, 1:].astype(BF)
     sends.start(gnear.at[:, 1], brecv, near_recv.at[0], partner, h)
-    w_ring(2)
-    open_ring(0)
-    backward_pick(1, rowdot)
-    share_picks(1)
-    sum_ring(0, 0)
+    open_ring(1)
+    sum_ring(0, 1)
+    backward_near(0, 0, 1)
+    arrived(brecv, near_recv.at[0], send.at[0], partner, h)
+    extra = brecv[...].astype(F32)
+    csum[...] = (gnear[:, 2].astype(F32) + jnp.where(core == 1, extra, 0.0)).astype(BF)
+    sends.start(csum, crecv, near_recv.at[1], before, h)
+    backward_near(1, 0, 1)
+    sum_ring(1, 0)
     arrived(wdown.at[2], wdown_recv.at[2], send.at[0], above, h)
     arrived(wup.at[3], wup_recv.at[3], send.at[0], below, h)
     wdone[...] = (wts[z, core].astype(F32) + wup[3].astype(F32)
                   + wdown[2].astype(F32)).astype(BF)
     sends.start(wdone.at[1 - yh], wslot, y_recv.at[2], ypeer, h)
-    open_ring(1)
-    arrived(brecv, near_recv.at[0], send.at[0], partner, h)
-    extra = brecv[...].astype(F32)
-    csum[...] = (gnear[:, 2].astype(F32) + jnp.where(core == 1, extra, 0.0)).astype(BF)
-    sends.start(csum, crecv, near_recv.at[1], before, h)
-    sum_ring(0, 1)
     for peer in hs:
         arrived(piece(core, peer), w_recv.at[core, peer], send.at[0], c, peer)
         sends.start(piece(core, peer), piece(core, peer), w_recv.at[core, peer], partner, h)
-    sum_ring(1, 0)
+    for r in range(2):
+        gq_ref[:, r * DH:(r + 1) * DH] = (acc[r].T * SCALE).astype(BF)
     sum_ring(0, 2)
     relay(west, 1, west)
     relay(east, 0, east)
@@ -438,21 +454,21 @@
     close_ring(0)
     for peer in hs:
         arrived(piece(1 - core, peer), w_recv.at[1 - core, peer], send.at[0], partner, h)
-    scores[0] = jnp.zeros((T, T), F32)
+    scores[0, 0] = jnp.zeros((T, T), F32)
 
     def project(r, _):
-        scores[0] += tn(att_all[r], wc[pl.ds(pl.multiple_of(r * 256, 256), 256), :])
+        scores[0, 0] += tn(att_all[r], wc[pl.ds(pl.multiple_of(r * 256, 256), 256), :])
         return 0
 
     lax.fori_loop(0, 4, project, 0)
     sum_ring(1, 2)
     lax.fori_loop(4, NH, project, 0)
     close_ring(1)
-    lo_ref[...] = scores[0].astype(BF)
+    lo_ref[...] = scores[0, 0].astype(BF)
     arrived(wslot, y_recv.at[2], send.at[0], ypeer, h)
     gw_ref[...] = (wdone[yh].astype(F32) + wslot[...].astype(F32)).astype(BF)
     arrived(crecv, near_recv.at[1], send.at[0], after, h)
-    grad = gnear[:, 0].astype(F32) + jnp.where(core == 1, 0.0, extra) + crecv[...].astype(F32)
+    grad = dnear[:, 0] + jnp.where(core == 1, 0.0, extra) + crecv[...].astype(F32)
     block = lax.broadcasted_iota(jnp.int32, (T, DH), 0) // BLK
     grads_out = [grad[0], grad[1]]
     for r in range(2):
@@ -499,9 +515,9 @@
         scratch_shapes=[
             buf(4, NC, BLK, DH), buf(2, 3, T, DH), buf(NH, T, T), buf(NH, 256, T),
             buf(2048, T), buf(2, 2, 16, 2, BLK, DH), buf(2, 3, T, DH),
-            buf(2, T, DH), buf(7, T, T, dtype=F32), buf(2, 7, T, T),
-            buf(2, 3, T, DH, dtype=F32), buf(8, T, dtype=F32), buf(2, 8, T, dtype=F32),
-            buf(DH, T, dtype=F32), buf(T, DH), buf(256, T, dtype=F32),
+            buf(2, T, DH), buf(2, 7, T, T, dtype=F32), buf(2, 7, T, T),
+            buf(2, 3, T, DH, dtype=F32), buf(2, 8, T, dtype=F32), buf(2, 8, T, dtype=F32),
+            buf(2, DH, T, dtype=F32), buf(2, T, DH), buf(256, T, dtype=F32), buf(2, 8, T, dtype=F32),
             buf(8, 2, 2, 256, DH), buf(8, 2, 256, DH), buf(4, 2, 256, DH), buf(3, 2, 256, DH),
             buf(2, 256, DH), buf(256, DH),
             buf(2, 8, 2, 2, BLK, DH), buf(2, 8, 2, DH, DH), buf(2, 4, 2, DH, DH),

time: 105 us -> 100 us (0.952)
  Pallas kernels: 104 us -> 99.4 us
    pallas_call x1, Pallas kernels: 102 us -> 97.2 us  [body(): pl.pallas_call(step_kernel, out_shape=shapes, in_specs=[SM, VM, VM, VM, V...]
where the time goes in v3:
time: 100 us
  Pallas kernels  99.4 us (99%)
    pallas_call x1, Pallas kernels, body(): pl.pallas_call(step_kernel, out_shape=shapes, in_specs=[SM, VM, VM, VM, V...  97.2 us
    pallas_call x1, Pallas kernels, body(): pl.pallas_call(hand_over, out_shape=shapes, in_specs=[VM] * 5, out_specs=...  2.2 us

profile of v3, /device:TPU:14, one launch (start us, length us, event | category | flops | bytes accessed | tf_op | source)
XLA Modules:
  0.0 100.0 jit_solution(7252867922087697359)
XLA Ops:
  0.6 97.2 %step.1 = (bf16[512,512]{1,0:T(8,128)(2,1)}, bf16[512,256]{1,0:T(8,128)(2,1)}, bf16[512,128]{1,0:T(8,128)(2,1)}, bf16[512,128]{1,0:T(8,128)(2,1)}, bf16[256,128]{1,0:T(8,128)(2,1)}) custom-call(s32[2]{0:T(128)} %off_ref.1, bf16[512,256]{1,0:T(8,128)(2,1)} %q_ref.1, bf16[512,128]{1,0:T(8,128)(2,1)} %k_ref.1, bf16[512,128]{1,0:T(8,128)(2,1)} %v_ref.1, ...), custom_call_target="tpu_custom_call" | custom-call | tf_op jit(solution)/shard_map/step/pallas_call | solution.py:510
  97.8 2.2 %hand_over.1 = (bf16[512,512]{1,0:T(8,128)(2,1)}, bf16[512,256]{1,0:T(8,128)(2,1)}, bf16[512,128]{1,0:T(8,128)(2,1)}, bf16[512,128]{1,0:T(8,128)(2,1)}, bf16[256,128]{1,0:T(8,128)(2,1)}) custom-call(bf16[512,512]{1,0:T(8,128)(2,1)} %get-tuple-element.10.refs_0_, bf16[512,256]{1,0:T(8,128)(2,1)} %get-tuple-element.11.refs_1_, ...), custom_call_target="tpu_custom_call" | custom-call | tf_op jit(solution)/shard_map/hand_over/pallas_call | solution.py:533

commit v4 on v3

--- a/solution.py
+++ b/solution.py
@@ -429,19 +429,18 @@
     extra = brecv[...].astype(F32)
     csum[...] = (gnear[:, 2].astype(F32) + jnp.where(core == 1, extra, 0.0)).astype(BF)
     sends.start(csum, crecv, near_recv.at[1], before, h)
+    sum_ring(1, 0)
     backward_near(1, 0, 1)
-    sum_ring(1, 0)
     arrived(wdown.at[2], wdown_recv.at[2], send.at[0], above, h)
     arrived(wup.at[3], wup_recv.at[3], send.at[0], below, h)
     wdone[...] = (wts[z, core].astype(F32) + wup[3].astype(F32)
                   + wdown[2].astype(F32)).astype(BF)
     sends.start(wdone.at[1 - yh], wslot, y_recv.at[2], ypeer, h)
-    for peer in hs:
-        arrived(piece(core, peer), w_recv.at[core, peer], send.at[0], c, peer)
-        sends.start(piece(core, peer), piece(core, peer), w_recv.at[core, peer], partner, h)
     for r in range(2):
         gq_ref[:, r * DH:(r + 1) * DH] = (acc[r].T * SCALE).astype(BF)
     sum_ring(0, 2)
+    sum_ring(1, 1)
+    close_ring(0)
     relay(west, 1, west)
     relay(east, 0, east)
     relay(west_side, 1, west)
@@ -450,8 +449,11 @@
     relay(far, 1, east)
     relay(far_side, 0, west)
     relay(far_side, 1, east)
-    sum_ring(1, 1)
-    close_ring(0)
+    for peer in hs:
+        arrived(piece(core, peer), w_recv.at[core, peer], send.at[0], c, peer)
+        sends.start(piece(core, peer), piece(core, peer), w_recv.at[core, peer], partner, h)
+    sum_ring(1, 2)
+    close_ring(1)
     for peer in hs:
         arrived(piece(1 - core, peer), w_recv.at[1 - core, peer], send.at[0], partner, h)
     scores[0, 0] = jnp.zeros((T, T), F32)
@@ -460,10 +462,7 @@
         scores[0, 0] += tn(att_all[r], wc[pl.ds(pl.multiple_of(r * 256, 256), 256), :])
         return 0
 
-    lax.fori_loop(0, 4, project, 0)
-    sum_ring(1, 2)
-    lax.fori_loop(4, NH, project, 0)
-    close_ring(1)
+    lax.fori_loop(0, NH, project, 0)
     lo_ref[...] = scores[0, 0].astype(BF)
     arrived(wslot, y_recv.at[2], send.at[0], ypeer, h)
     gw_ref[...] = (wdone[yh].astype(F32) + wslot[...].astype(F32)).astype(BF)

time: 100 us -> 100 us (level)
  no operation moved by 1% of the time
where the time goes in v4:
time: 100 us; the launch traced here: 99.9 us
  Pallas kernels  99.3 us (99%)
    pallas_call x1, Pallas kernels, body(): pl.pallas_call(step_kernel, out_shape=shapes, in_specs=[SM, VM, VM, VM, V...  97.1 us
    pallas_call x1, Pallas kernels, body(): pl.pallas_call(hand_over, out_shape=shapes, in_specs=[VM] * 5, out_specs=...  2.2 us

profile of v4, /device:TPU:14, one launch (start us, length us, event | category | flops | bytes accessed | tf_op | source)
XLA Modules:
  0.0 99.9 jit_solution(18404034517588922868)
XLA Ops:
  0.6 97.1 %step.1 = (bf16[512,512]{1,0:T(8,128)(2,1)}, bf16[512,256]{1,0:T(8,128)(2,1)}, bf16[512,128]{1,0:T(8,128)(2,1)}, bf16[512,128]{1,0:T(8,128)(2,1)}, bf16[256,128]{1,0:T(8,128)(2,1)}) custom-call(s32[2]{0:T(128)} %off_ref.1, bf16[512,256]{1,0:T(8,128)(2,1)} %q_ref.1, bf16[512,128]{1,0:T(8,128)(2,1)} %k_ref.1, bf16[512,128]{1,0:T(8,128)(2,1)} %v_ref.1, ...), custom_call_target="tpu_custom_call" | custom-call | tf_op jit(solution)/shard_map/step/pallas_call | solution.py:509
  97.7 2.2 %hand_over.1 = (bf16[512,512]{1,0:T(8,128)(2,1)}, bf16[512,256]{1,0:T(8,128)(2,1)}, bf16[512,128]{1,0:T(8,128)(2,1)}, bf16[512,128]{1,0:T(8,128)(2,1)}, bf16[256,128]{1,0:T(8,128)(2,1)}) custom-call(bf16[512,512]{1,0:T(8,128)(2,1)} %get-tuple-element.10.refs_0_, bf16[512,256]{1,0:T(8,128)(2,1)} %get-tuple-element.11.refs_1_, ...), custom_call_target="tpu_custom_call" | custom-call | tf_op jit(solution)/shard_map/hand_over/pallas_call | solution.py:532
